TPU v7x, 32 devices: a whole 2x2x4 slice. The times are simulated.
32 devices in a mesh: grp: 2 (over x), space: 16 (over z, y, core).
Axes of the slice: x: 2, y: 2, z: 4, core: 2. Of those that a mesh axis runs over, the one named last changes fastest.
Arguments:
- right_side: float32 [165, 12288], P(None, ('grp', 'space')), parts along dimension 1, may hold values from -48 to 48
- capacity: float32 [12288], P(('grp', 'space')), parts along dimension 0, may hold values from 0.5 to 2
- base_cond: float32 [192, 24, 4096], P(('grp', 'space')), parts along dimension 0, may hold values from 0.0005 to 0.005
- var_field: float32 [8, 12288], P(None, ('grp', 'space')), parts along dimension 1, may hold values from -1 to 1
- block_cols: int32 [192, 23], P(('grp', 'space')), parts along dimension 0, may hold values from 0 to 11, as said below
- send_list: int32 [32, 2, 3], P(('grp', 'space')), parts along dimension 0, may hold values from 0 to 5, as said below
Outputs:
- solution_field: float32 [165, 12288], P(None, ('grp', 'space')), parts along dimension 1
- residual: float32 [165, 12288], P(None, ('grp', 'space')), parts along dimension 1
There are 2 independent parts, one for each index of `grp`. A program takes and returns all parts, laid end to end along the dimension named above; each array names one. Nothing has to cross between parts.
Inputs may be any that keep to these rules, and one draw needn't show every extreme that they name: `block_cols`: A value below 6 names a block of the same device; 6 + h names the h-th block that the previous device of space sends up, 9 + h the h-th block that the next device sends down. The first device never names the previous one, the last never names the next one; every other value occurs on every device. `send_list`: on every device the 6 blocks differ; block 5 is always sent up and block 0 always sent down.
All inputs are finite; a program needn't handle non-finite values.
Results may differ from a plain program's by a relative error of at most 0.0003.
Values sent between devices are 32-bit elements; how exact they have to be, the bound alone decides.
No kernel may reach another device: no remote copies, remote signals or barrier semaphores. Data moves between devices by JAX's collectives and lax.ppermute only.
A program may use at most 128 MiB of HBM per device.

v0:
```python
import functools
import math

import jax
import jax.numpy as jnp
from jax import lax
from jax.experimental import pallas as pl
from jax.experimental.pallas import tpu as pltpu
from jax.sharding import PartitionSpec as P

VARS = 8
ORDER = 3
LANES = 128
SPREAD = 0.14
F32 = jnp.float32
BF16 = jnp.bfloat16


@functools.cache
def chaos_links():
    entries = []

    def grow(prefix, budget_left):
        if len(prefix) == VARS:
            entries.append(tuple(prefix))
            return
        for degree in range(budget_left + 1):
            grow(prefix + [degree], budget_left - degree)

    grow([], ORDER)
    entries.sort(key=lambda beta: (sum(beta), tuple(-v for v in beta)))
    lookup = {beta: place for place, beta in enumerate(entries)}
    links = []
    for beta in entries:
        mine = []
        for k in range(VARS):
            if beta[k] > 0:
                lowered = beta[:k] + (beta[k] - 1,) + beta[k + 1 :]
                mine.append((k, lookup[lowered], beta[k]))
            raised = beta[:k] + (beta[k] + 1,) + beta[k + 1 :]
            if raised in lookup:
                mine.append((k, lookup[raised], beta[k] + 1))
        links.append(mine)
    return links


def split(value):
    high = value.astype(BF16)
    return high, (value - high.astype(F32)).astype(BF16)


def product(high, low, w_high, w_low, dims):
    rows = high.shape[0]
    both = jnp.concatenate([high, low], axis=0)
    dot = functools.partial(lax.dot_general, dimension_numbers=(dims, ((), ())), preferred_element_type=F32)
    main = dot(both, w_high)
    return main[:rows] + (main[rows:] + dot(high, w_low))


def couple(source, target, coefs, part=0, parts=1):
    first = coefs[0]
    scaled = {}
    for k in range(VARS):
        for square in range(1, ORDER + 1):
            scaled[k, square] = coefs[k + 1] if square == 1 else coefs[k + 1] * math.sqrt(square)
    links = chaos_links()
    for term in range(part * len(links) // parts, (part + 1) * len(links) // parts):
        mine = links[term]
        total = source[term * 8 : term * 8 + 8, :]
        if first is not None:
            total = total * first
        for k, other, square in mine:
            total = total + scaled[k, square] * source[other * 8 : other * 8 + 8, :]
        target[term * 8 : term * 8 + 8, :] = total


def spread_rows(target, chunk, value):
    target[pl.ds(chunk, value.shape[0], stride=8), :] = value


def lane_iota(shape):
    return lax.broadcasted_iota(jnp.int32, shape, len(shape) - 1)


def row_iota(shape):
    return lax.broadcasted_iota(jnp.int32, shape, 0)


def pick_block(ref, place, half, rows):
    tile = ref[0:rows, pl.ds(pl.multiple_of((place // 2) * LANES, LANES), LANES)]
    return jnp.where(place % 2 == half, tile, pltpu.roll(tile, LANES // 2, 1))


def permute_blocks(ref, places, chunk, rows):
    left = pick_block(ref, places[2 * chunk], 0, rows)
    right = pick_block(ref, places[2 * chunk + 1], 1, rows)
    return jnp.where(lane_iota(left.shape) < LANES // 2, left, right)


def marked(value, terms):
    row = row_iota(value.shape)
    return jnp.where(row < terms, value, jnp.where(row == terms, 1.0, 0.0))


def lower_half(value):
    return lane_iota(value.shape) < value.shape[1] // 2


def by_side(near, far):
    place, count = lax.axis_index("space"), lax.axis_size("space")
    far = jnp.where((place == 0) | (place == count - 1), 0.0, far)
    even = place % 2 == 0
    return jnp.where(even, far, near), jnp.where(even, near, far)


def store_sides(near, far, up, down):
    even = lax.axis_index("space") % 2 == 0
    near[...] = jnp.where(even, up, down)
    far[...] = jnp.where(even, down, up)


def transpose8(tiles):
    tiles = [tile if t == 0 else pltpu.roll(tile, t, 0) for t, tile in enumerate(tiles)]
    row = row_iota(tiles[0].shape)
    for bit in (1, 2, 4):
        take = row & bit != 0
        tiles = [jnp.where(take, tiles[(t + bit) % 8], tiles[t]) for t in range(8)]
    return [tiles[0] if k == 0 else pltpu.roll(tiles[8 - k], 8 - k, 0) for k in range(8)]


def to_terms(target, *values):
    tiles = [(value, lane) for value in values for lane in range(0, value.shape[1], LANES)]
    for chunk, (value, lane) in enumerate(tiles):
        spread_rows(target, chunk, value[:, lane : lane + LANES])


def from_terms(source, count):
    rows = source.shape[0] // 8
    return [
        jnp.concatenate([source[pl.ds(3 * i + chunk, rows, stride=8), :] for chunk in range(3)], axis=1)
        for i in range(count)
    ]


def coef_list(ref):
    return [ref[k * 8 : k * 8 + 8, :] for k in range(VARS + 1)]


def set_coefs(ref, first, leading, rest):
    for chunk in range(leading.shape[1] // LANES):
        lanes = slice(chunk * LANES, (chunk + 1) * LANES)
        ref[first + chunk : first + chunk + 1, :] = leading[:, lanes]
        ref[pl.ds(8 + first + chunk, VARS, stride=8), :] = rest[:, lanes]


def lane_dot(a, b):
    lanes_sum = jnp.sum(a * b, axis=0, keepdims=True)
    total = lanes_sum[:, 0:LANES]
    for start in range(LANES, a.shape[1], LANES):
        total = total + lanes_sum[:, start : start + LANES]
    return total


def order_of(sends):
    halves = sends.shape[2]
    return [sends[0, j // halves, j % halves] for j in range(2 * halves)]


def send_kernel(sends_in, field_in, field_p, near, far, sends, field, sems):
    terms, nodes = field_in.shape
    tall = field_p.shape[0]
    copies = [
        pltpu.make_async_copy(sends_in, sends, sems.at[0]),
        pltpu.make_async_copy(field_in, field, sems.at[1]),
    ]
    for copy in copies:
        copy.start()
    for copy in copies:
        copy.wait()
    order = order_of(sends)
    for chunk in range(nodes // LANES):
        lanes = slice(chunk * LANES, (chunk + 1) * LANES)
        field_p[0:terms, lanes] = permute_blocks(field, order, chunk, terms)
        field_p[terms:tall, lanes] = jnp.zeros((tall - terms, LANES), F32)
    value = field_p[...]
    store_sides(near, far, value[:, : nodes - LANES], value[:, LANES:])


def build_kernel(
    sends_in, cols_in, cap_in, var_in, base, field_p,
    w_high, w_low, part, near_own, flux_out, coef_own, coef_halo, cap_p,
    buf, acc, dense, major, result, weights_p, sends, cols, cap, var, place, sems,
):
    blocks, slots, flat = base.shape
    tall, nodes = field_p.shape
    terms = len(chaos_links())
    width = nodes // blocks
    steps = flat // LANES
    chunks = nodes // LANES
    small = [
        pltpu.make_async_copy(source, target, sems.at[blocks + i])
        for i, (source, target) in enumerate(
            ((sends_in, sends), (cols_in, cols), (cap_in, cap.at[0]), (var_in, var))
        )
    ]
    for copy in small:
        copy.start()
    copies = [pltpu.make_async_copy(base.at[j], buf.at[j], sems.at[j]) for j in range(blocks)]
    for copy in copies:
        copy.start()
    for copy in small:
        copy.wait()
    order = order_of(sends)
    for j in range(2 * blocks):
        place[j] = j
    for j in range(blocks):
        place[order[j]] = j

    for chunk in range(chunks):
        lanes = slice(chunk * LANES, (chunk + 1) * LANES)
        weights_p[:, lanes] = permute_blocks(var, order, chunk, VARS) * SPREAD
        cap_p[:, lanes] = permute_blocks(cap, order, chunk, 1)
    weights = weights_p[...]
    value = field_p[...]
    for coef in (coef_own, coef_halo):
        coef[...] = jnp.zeros_like(coef)
        set_coefs(coef, 0, jnp.ones((1, nodes), F32), weights)
    to_terms(major, value, value)
    couple(major, result, coef_list(coef_own))

    for one in acc:
        one[...] = jnp.zeros_like(one)
    for copy in copies:
        copy.wait()
    for slot in range(0, slots, 8):
        for j in range(blocks):
            spots = [j if s == 0 else place[cols[order[j], s - 1]] for s in range(slot, slot + 8)]
            for step in range(0, steps, 8):
                tiles = [
                    buf[order[j], slot : slot + 8, t * LANES : (t + 1) * LANES] for t in range(step, step + 8)
                ]
                for spot, tile in zip(spots, transpose8(tiles)):
                    acc[j][spot, step : step + 8, :] += tile
    row = row_iota((8, LANES))
    near = lane_iota((8, LANES)) < width
    for j in range(blocks):
        for pair in range(blocks):
            lanes = slice(pair * LANES, (pair + 1) * LANES)
            for step in range(0, steps, 8):
                even = acc[j][2 * pair, step : step + 8, :]
                odd = acc[j][2 * pair + 1, step : step + 8, :]
                first = jnp.where(near, even, pltpu.roll(odd, width, 1))
                second = jnp.where(near, pltpu.roll(even, width, 1), odd)
                for half in range(2):
                    pick = row // 2 + 4 * half
                    start = j * width + 2 * step + 8 * half
                    dense[start : start + 8, lanes] = jnp.where(
                        row % 2 == 0,
                        jnp.take_along_axis(first, pick, axis=0),
                        jnp.take_along_axis(second, pick, axis=0),
                    )
    for pair in range(blocks):
        lanes = slice(pair * LANES, (pair + 1) * LANES)
        w_high[:, lanes], w_low[:, lanes] = split(dense[:, lanes])

    left = jnp.concatenate([marked(from_terms(result, 1)[0], terms), weights], axis=0)
    flux = product(*split(left), w_high[...], w_low[...], ((1,), (0,)))
    for coef, first, lanes in ((coef_own, chunks, slice(0, nodes)), (coef_halo, chunks, slice(nodes, 2 * nodes))):
        set_coefs(coef, first, flux[terms : terms + 1, lanes], flux[tall : tall + VARS, lanes])
    flux_out[...] = flux[0:tall, nodes:]
    near_own[...] = product(
        *split(marked(value, terms)), w_high[:, 0:nodes], w_low[:, 0:nodes], ((1,), (1,))
    )
    couple(major, result, coef_list(coef_own))
    part[...] = cap_p[...] * value + from_terms(result, 2)[1] - flux[0:tall, 0:nodes]


def local_kernel(
    w_high, w_low, field, part, near_own, flux_halo, coef_halo, got_near, got_far,
    local, halo_flux, near, far, major, result,
):
    tall, nodes = field.shape
    terms = len(chaos_links())
    below, above = by_side(got_near[...], got_far[...])
    gap = jnp.zeros((tall, LANES), F32)
    halo = jnp.concatenate([below, gap], axis=1)
    halo = jnp.where(lower_half(halo), halo, jnp.concatenate([gap, above], axis=1))
    value = field[...]
    row = row_iota(value.shape)
    mixed = near_own[...] + product(
        *split(marked(halo, terms)), w_high[:, nodes:], w_low[:, nodes:], ((1,), (1,))
    )
    to_terms(major, mixed[terms : terms + 1, :] * value - mixed, halo)
    couple(major, result, coef_list(coef_halo))
    forward, outer = from_terms(result, 2)
    own = jnp.where(row < terms, part[...] + forward, 0.0)
    outer = jnp.where(row < terms, outer - flux_halo[...], 0.0)
    local[...] = own
    halo_flux[...] = outer
    half = lower_half(own)
    store_sides(near, far, jnp.where(half, own, outer), jnp.where(half, outer, own))


def second_kernel(
    peers,
    w_high, w_low, field, local, halo_flux, cap, coef_own, coef_halo, got_near, got_far,
    image, local2, near, far, dots, major, result, major2, result2,
):
    _, nodes = field.shape
    terms = len(chaos_links())
    below, above = by_side(got_near[...], got_far[...])
    half = lower_half(below)
    row = row_iota(below.shape)
    value = jnp.where(row < terms, local[...] + jnp.where(half, above, below), 0.0)
    halo = jnp.where(row < terms, halo_flux[...] + jnp.where(half, below, above), 0.0)
    image[...] = value
    to_terms(major, value, value)
    extended = split(marked(jnp.concatenate([value, halo], axis=1), terms))
    coefs = coef_list(coef_own)
    mixed = []
    cuts = list(range(0, nodes, 2 * LANES))
    for part, start in enumerate(cuts):
        span = slice(start, min(start + 2 * LANES, nodes))
        mixed.append(product(*extended, w_high[span, :], w_low[span, :], ((1,), (1,))))
        couple(major, result, coefs, part, len(cuts))
    mixed = jnp.concatenate(mixed, axis=1)
    to_terms(major2, mixed[terms : terms + 1, :] * value - mixed, halo)
    coupled, transferred = from_terms(result, 2)
    coupled = split(jnp.where(row < terms, coupled, 0.0))
    coefs = coef_list(coef_halo)
    flux = []
    cuts = list(range(0, 2 * nodes, 2 * LANES))
    for part, start in enumerate(cuts):
        span = slice(start, start + 2 * LANES)
        flux.append(product(*coupled, w_high[:, span], w_low[:, span], ((1,), (0,))))
        couple(major2, result2, coefs, part, len(cuts))
    flux = jnp.concatenate(flux, axis=1)
    forward, outer = from_terms(result2, 2)
    own = cap[...] * value + transferred + forward - flux[:, 0:nodes]
    own = jnp.where(row < terms, own, 0.0)
    outer = outer - flux[:, nodes:]
    outer = jnp.where(row < terms, outer, 0.0)
    local2[...] = own
    store_sides(near, far, outer[:, LANES:], outer[:, : nodes - LANES])
    sums = [
        lane_dot(field[...], field[...]),
        lane_dot(field[...], value),
        lane_dot(value, value),
        lane_dot(value, own) + lane_dot(halo, outer),
    ]
    lane = lane_iota((1, LANES))
    packed = jnp.zeros((1, LANES), F32)
    for k, one in enumerate(sums):
        one = one + pltpu.roll(one, LANES // 2, 1)
        one = one + pltpu.roll(one, LANES // 4, 1)
        packed = jnp.where(lane // (LANES // 4) == k, one, packed)
    for peer in range(peers):
        dots[peer] = packed


def final_kernel(
    peers, sends, dots, field, image, local2, got_near, got_far,
    solution_out, residual_out, place, work, out, sems,
):
    terms, nodes = solution_out.shape
    tall = field.shape[0]
    order = order_of(sends)
    blocks = len(order)
    for j in range(blocks):
        place[order[j]] = j
    places = [place[j] for j in range(blocks)]
    total = dots[0]
    for peer in range(1, peers):
        total = total + dots[peer]
    quarter = lane_iota(total.shape) < LANES // 4

    def add(row):
        return jnp.sum(jnp.where(quarter, row, 0.0), axis=1, keepdims=True)

    bb, by, yy, yz = [total] + [pltpu.roll(total, LANES - k * LANES // 4, 1) for k in range(1, 4)]
    norm = add(bb)
    step0 = norm / add(by)
    norm1 = add(bb - step0 * (2.0 * by - step0 * yy))
    ratio = norm1 / norm
    grow = 1.0 + ratio
    curve = add(grow * grow * by - step0 * (grow * (2.0 * yy) - step0 * yz))
    step1 = norm1 / curve
    c1 = step0 + step1 * grow
    c2 = step0 * step1
    copies = []

    def put(which, target):
        for chunk in range(nodes // LANES):
            lanes = slice(chunk * LANES, (chunk + 1) * LANES)
            out[which, :, lanes] = permute_blocks(work.at[which], places, chunk, terms)
        copies.append(pltpu.make_async_copy(out.at[which], target, sems.at[which]))
        copies[-1].start()

    work[0] = c1 * field[...] - c2 * image[...]
    put(0, solution_out)
    below, above = by_side(got_near[...], got_far[...])
    gap = jnp.zeros((tall, LANES), F32)
    inward = jnp.concatenate([above, gap], axis=1)
    inward = jnp.where(lower_half(inward), inward, jnp.concatenate([gap, below], axis=1))
    work[1] = field[...] - c1 * image[...] + c2 * (local2[...] + inward)
    put(1, residual_out)
    for copy in copies:
        copy.wait()


def vmem(count):
    return [pl.BlockSpec(memory_space=pltpu.VMEM)] * count


def hbm(count):
    return [pl.BlockSpec(memory_space=pltpu.HBM)] * count


def smem(count):
    return [pl.BlockSpec(memory_space=pltpu.SMEM)] * count


def in_hbm(value):
    return pltpu.with_memory_space_constraint(value, pltpu.HBM)


def shape(dims, dtype=F32):
    return jax.ShapeDtypeStruct(dims, dtype)


def exchange(near, far):
    count, groups = lax.axis_size("space"), lax.axis_size("grp")
    outer = []
    for group in range(groups):
        start = group * count
        outer += [(start + i, start + (i + 1 if i % 2 else i - 1)) for i in range(1, count - 1)]
        mate = (group ^ 1 if groups % 2 == 0 else group) * count
        ends = (0, count - 1) if groups % 2 == 0 else (count - 1, 0)
        outer += [(start, mate + ends[0]), (start + count - 1, mate + ends[1])]
    inner = [(i, i ^ 1) for i in range(count)]
    got_far = lax.ppermute(far, ("grp", "space"), outer)
    got_near = lax.ppermute(near, "space", inner)
    return got_near, got_far


def shards(right_side, capacity, base_cond, var_field, block_cols, send_list):
    blocks, slots, flat = base_cond.shape
    terms, nodes = right_side.shape
    peers = lax.axis_size("space")
    tall = -(-terms // 8) * 8
    steps = flat // LANES
    params = pltpu.CompilerParams(vmem_limit_bytes=48 * 1024 * 1024)
    wide = shape((tall, nodes))
    piece = shape((tall, nodes - LANES))
    coefs = shape((8 * (VARS + 1), LANES))
    weights = shape((nodes, 2 * nodes), BF16)
    spread = pltpu.VMEM((tall * 8, LANES), F32)
    sends = in_hbm(send_list)

    field, near, far = pl.pallas_call(
        send_kernel,
        out_shape=(wide, piece, piece),
        in_specs=hbm(2),
        out_specs=tuple(vmem(3)),
        scratch_shapes=[
            pltpu.SMEM(send_list.shape, jnp.int32),
            pltpu.VMEM((terms, nodes), F32),
            pltpu.SemaphoreType.DMA((2,)),
        ],
        compiler_params=params,
        name="send",
    )(sends, in_hbm(right_side))
    got = exchange(near, far)

    w_high, w_low, part, near_own, flux_halo, coef_own, coef_halo, cap = pl.pallas_call(
        build_kernel,
        out_shape=(weights, weights, wide, wide, wide, coefs, coefs, shape((1, nodes))),
        in_specs=hbm(5) + vmem(1),
        out_specs=tuple(vmem(8)),
        scratch_shapes=[
            pltpu.VMEM((blocks, slots, flat), F32),
            [pltpu.VMEM((2 * blocks, steps, LANES), F32) for _ in range(blocks)],
            pltpu.VMEM((nodes, 2 * nodes), F32),
            spread,
            spread,
            pltpu.VMEM((VARS, nodes), F32),
            pltpu.SMEM(send_list.shape, jnp.int32),
            pltpu.SMEM(block_cols.shape, jnp.int32),
            pltpu.VMEM((1, nodes), F32),
            pltpu.VMEM((VARS, nodes), F32),
            pltpu.SMEM((2 * blocks,), jnp.int32),
            pltpu.SemaphoreType.DMA((blocks + 4,)),
        ],
        compiler_params=params,
        cost_estimate=pl.CostEstimate(flops=10**9, bytes_accessed=4 * 10**6, transcendentals=0),
        name="build",
    )(sends, in_hbm(block_cols), in_hbm(capacity), in_hbm(var_field), in_hbm(base_cond), field)

    local, halo_flux, near, far = pl.pallas_call(
        local_kernel,
        out_shape=(wide, wide, wide, wide),
        in_specs=vmem(9),
        out_specs=tuple(vmem(4)),
        scratch_shapes=[spread] * 2,
        compiler_params=params,
        name="local",
    )(w_high, w_low, field, part, near_own, flux_halo, coef_halo, *got)
    got = exchange(near, far)

    image, local2, near, far, dots = pl.pallas_call(
        functools.partial(second_kernel, peers),
        out_shape=(wide, wide, piece, piece, shape((peers, 1, LANES))),
        in_specs=vmem(10),
        out_specs=tuple(vmem(5)),
        scratch_shapes=[spread] * 4,
        compiler_params=params,
        name="second",
    )(w_high, w_low, field, local, halo_flux, cap, coef_own, coef_halo, *got)
    got = exchange(near, far)
    gathered = lax.all_to_all(dots, "space", 0, 0, tiled=True)

    return pl.pallas_call(
        functools.partial(final_kernel, peers),
        out_shape=(shape((terms, nodes)), shape((terms, nodes))),
        in_specs=smem(1) + vmem(6),
        out_specs=tuple(hbm(2)),
        scratch_shapes=[
            pltpu.SMEM((2 * blocks,), jnp.int32),
            pltpu.VMEM((2, tall, nodes), F32),
            pltpu.VMEM((2, terms, nodes), F32),
            pltpu.SemaphoreType.DMA((2,)),
        ],
        compiler_params=params,
        name="finish",
    )(send_list, gathered, field, image, local2, *got)


def solution(mesh):
    return jax.shard_map(
        shards,
        mesh=mesh,
        in_specs=(
            P(None, ("grp", "space")),
            P(("grp", "space")),
            P(("grp", "space"), None, None),
            P(None, ("grp", "space")),
            P(("grp", "space"), None),
            P(("grp", "space"), None, None),
        ),
        out_specs=(P(None, ("grp", "space")), P(None, ("grp", "space"))),
        check_vma=False,
    )
```

profile of v0, /device:TPU:0, one launch (start us, length us, event | category | flops | bytes accessed | tf_op | source)
XLA Modules:
  0.0 36.5 jit_solution(4247065713340996178)
XLA Ops:
  0.6 1.2 %send.1 = (f32[168,384]{1,0:T(8,128)S(1)}, f32[168,256]{1,0:T(8,128)S(1)}, f32[168,256]{1,0:T(8,128)S(1)}) custom-call(s32[1,2,3]{2,1,0:T(2,128)} %sends.1, f32[165,384]{1,0:T(8,128)} %field_in.1), custom_call_target="tpu_custom_call" | custom-call | tf_op jit(solution)/shard_map/send/pallas_call | solution.py:460
  1.8 0.6 %collective-permute-start = (f32[168,256]{1,0:T(8,128)S(1)}, f32[168,256]{1,0:T(8,128)S(1)}, u32[]{:S(2)}, u32[]{:S(2)}) collective-permute-start(f32[168,256]{1,0:T(8,128)S(1)} %get-tuple-element.29), channel_id=1, source_target_pairs={{0,1},{1,0},{2,3},{3,2},{4,5},{5,4},{6,7},{7,6},{8,9},{9,8},{10,11... | collective-permute-start | bytes 516104 | tf_op jit(solution)/shard_map/ppermute | solution.py:442
  2.4 2.6 %collective-permute-start.1 = (f32[168,256]{1,0:T(8,128)S(1)}, f32[168,256]{1,0:T(8,128)S(1)}, u32[]{:S(2)}, u32[]{:S(2)}) collective-permute-start(f32[168,256]{1,0:T(8,128)S(1)} %get-tuple-element.30), channel_id=1, source_target_pairs={{1,2},{2,1},{3,4},{4,3},{5,6},{6,5},{7,8},{8,7},{9,10},{10,9},{11,... | collective-permute-start | bytes 516104 | tf_op jit(solution)/shard_map/ppermute | solution.py:441
  4.9 3.7 %build.1 = (bf16[384,768]{1,0:T(8,128)(2,1)S(1)}, bf16[384,768]{1,0:T(8,128)(2,1)S(1)}, f32[168,384]{1,0:T(8,128)S(1)}, f32[168,384]{1,0:T(8,128)S(1)}, f32[168,...) custom-call(s32[1,2,3]{2,1,0:T(2,128)} %sends.1, s32[6,23]{1,0:T(8,128)} %cols_in.1, ...), custom_call_target="tpu_custom_call" | custom-call | flops 1000000000 | bytes 4000000 | tf_op jit(solution)/shard_map/build/pallas_call | solution.py:475
  8.7 0.0 collective-permute-done.got_near
  8.7 0.0 collective-permute-done.1.got_far
  8.7 0.0 copy-start
  8.7 1.0 %local.1 = (f32[168,384]{1,0:T(8,128)S(1)}, f32[168,384]{1,0:T(8,128)S(1)}, f32[168,384]{1,0:T(8,128)S(1)}, f32[168,384]{1,0:T(8,128)S(1)}) custom-call(bf16[384,768]{1,0:T(8,128)(2,1)S(1)} %get-tuple-element.23.w_high, bf16[384,768]{1,0:T(8,128)(2,1)S(1)} %get-tuple-element.24.w_low, f32[168,384]{1,0:T(8,128)S(1)} %get-tuple-element.22.field_p.field, ...), custom_call_target="tpu_custom_call" | custom-call | tf_op jit(solution)/shard_map/local/pallas_call | solution.py:499
  9.7 0.6 %collective-permute-start.2 = (f32[168,384]{1,0:T(8,128)S(1)}, f32[168,384]{1,0:T(8,128)S(1)}, u32[]{:S(2)}, u32[]{:S(2)}) collective-permute-start(f32[168,384]{1,0:T(8,128)S(1)} %get-tuple-element.35), channel_id=1, source_target_pairs={{0,1},{1,0},{2,3},{3,2},{4,5},{5,4},{6,7},{7,6},{8,9},{9,8},{10,11... | collective-permute-start | bytes 774152 | tf_op jit(solution)/shard_map/ppermute | solution.py:442
  10.3 1.5 %collective-permute-start.3 = (f32[168,384]{1,0:T(8,128)S(1)}, f32[168,384]{1,0:T(8,128)S(1)}, u32[]{:S(2)}, u32[]{:S(2)}) collective-permute-start(f32[168,384]{1,0:T(8,128)S(1)} %get-tuple-element.36), channel_id=1, source_target_pairs={{1,2},{2,1},{3,4},{4,3},{5,6},{6,5},{7,8},{8,7},{9,10},{10,9},{11,... | collective-permute-start | bytes 774152 | tf_op jit(solution)/shard_map/ppermute | solution.py:441
  11.8 0.0 collective-permute-done.2.got_near
  11.8 4.8 %collective-permute-done.3.got_far = f32[168,384]{1,0:T(8,128)S(1)} collective-permute-done((f32[168,384]{1,0:T(8,128)S(1)}, f32[168,384]{1,0:T(8,128)S(1)}, u32[]{:S(2)}, u32[]{:S(2)}) %collective-permute-start.3) | collective-permute-done | bytes 258080 | tf_op jit(solution)/shard_map/ppermute | solution.py:441
  16.6 1.8 %second.1 = (f32[168,384]{1,0:T(8,128)S(1)}, f32[168,384]{1,0:T(8,128)S(1)}, f32[168,256]{1,0:T(8,128)S(1)}, f32[168,256]{1,0:T(8,128)S(1)}, f32[16,1,128]{2,1,0:T(1,128)S(1)}) custom-call(bf16[384,768]{1,0:T(8,128)(2,1)S(1)} %get-tuple-element.23.w_high, bf16[384,768]{1,0:T(8,128)(2,1)S(1)} %get-tuple-element.24.w_low, ...), custom_call_target="tpu_custom_call" | custom-call | tf_op jit(solution)/shard_map/second/pallas_call | solution.py:510
  18.4 2.3 %collective-permute-start.4 = (f32[168,256]{1,0:T(8,128)S(1)}, f32[168,256]{1,0:T(8,128)S(1)}, u32[]{:S(2)}, u32[]{:S(2)}) collective-permute-start(f32[168,256]{1,0:T(8,128)S(1)} %get-tuple-element.40), channel_id=1, source_target_pairs={{0,1},{1,0},{2,3},{3,2},{4,5},{5,4},{6,7},{7,6},{8,9},{9,8},{10,11... | collective-permute-start | bytes 516104 | tf_op jit(solution)/shard_map/ppermute | solution.py:442
  20.7 1.5 %collective-permute-start.5 = (f32[168,256]{1,0:T(8,128)S(1)}, f32[168,256]{1,0:T(8,128)S(1)}, u32[]{:S(2)}, u32[]{:S(2)}) collective-permute-start(f32[168,256]{1,0:T(8,128)S(1)} %get-tuple-element.41), channel_id=1, source_target_pairs={{1,2},{2,1},{3,4},{4,3},{5,6},{6,5},{7,8},{8,7},{9,10},{10,9},{11,... | collective-permute-start | bytes 516104 | tf_op jit(solution)/shard_map/ppermute | solution.py:441
  22.2 12.2 %all_to_all.5.dots = f32[16,1,128]{2,1,0:T(1,128)S(1)} all-to-all(f32[16,1,128]{2,1,0:T(1,128)S(1)} %get-tuple-element.37), channel_id=1, replica_groups=mesh['grp'=2,'space'=16] {'space'}, dimensions={0} | all-to-all | bytes 16384 | tf_op jit(solution)/shard_map/all_to_all | solution.py:520
  34.4 0.0 collective-permute-done.4.got_near
  34.4 0.0 collective-permute-done.5.got_far
  34.4 0.0 copy-done
  34.4 2.1 %finish.1 = (f32[165,384]{1,0:T(8,128)}, f32[165,384]{1,0:T(8,128)}) custom-call(s32[1,2,3]{2,1,0:T(2,128)S(1)} %copy-done, f32[16,1,128]{2,1,0:T(1,128)S(1)} %all_to_all.5.dots, f32[168,384]{1,0:T(8,128)S(1)} %get-tuple-element.22.field_p.field, f32[168,384]{1,0:T(8,128)S(1)} %get-tuple-element.38.image, f32[168,384]{1,0:T(8,128)S(1)} %get-tuple-element.39.local2, ...), custom_call_target="tpu_custom_call" | custom-call | tf_op jit(solution)/shard_map/finish/pallas_call | solution.py:522
Async XLA Ops:
  1.8 6.9 %collective-permute-start = (f32[168,256]{1,0:T(8,128)S(1)}, f32[168,256]{1,0:T(8,128)S(1)}, u32[]{:S(2)}, u32[]{:S(2)}) collective-permute-start(f32[168,256]{1,0:T(8,128)S(1)} %get-tuple-element.29), channel_id=1, source_target_pairs={{0,1},{1,0},{2,3},{3,2},{4,5},{5,4},{6,7},{7,6},{8,9},{9,8},{10,11... | collective-permute-start | bytes 516104 | tf_op jit(solution)/shard_map/ppermute | solution.py:442
  2.4 6.3 %collective-permute-start.1 = (f32[168,256]{1,0:T(8,128)S(1)}, f32[168,256]{1,0:T(8,128)S(1)}, u32[]{:S(2)}, u32[]{:S(2)}) collective-permute-start(f32[168,256]{1,0:T(8,128)S(1)} %get-tuple-element.30), channel_id=1, source_target_pairs={{1,2},{2,1},{3,4},{4,3},{5,6},{6,5},{7,8},{8,7},{9,10},{10,9},{11,... | collective-permute-start | bytes 516104 | tf_op jit(solution)/shard_map/ppermute | solution.py:441
  8.7 25.7 %copy-start = (s32[1,2,3]{2,1,0:T(2,128)S(1)}, s32[1,2,3]{2,1,0:T(2,128)}, u32[]{:S(2)}) copy-start(s32[1,2,3]{2,1,0:T(2,128)} %sends.1) | copy-start | bytes 76
  9.7 2.1 %collective-permute-start.2 = (f32[168,384]{1,0:T(8,128)S(1)}, f32[168,384]{1,0:T(8,128)S(1)}, u32[]{:S(2)}, u32[]{:S(2)}) collective-permute-start(f32[168,384]{1,0:T(8,128)S(1)} %get-tuple-element.35), channel_id=1, source_target_pairs={{0,1},{1,0},{2,3},{3,2},{4,5},{5,4},{6,7},{7,6},{8,9},{9,8},{10,11... | collective-permute-start | bytes 774152 | tf_op jit(solution)/shard_map/ppermute | solution.py:442
  10.3 6.3 %collective-permute-start.3 = (f32[168,384]{1,0:T(8,128)S(1)}, f32[168,384]{1,0:T(8,128)S(1)}, u32[]{:S(2)}, u32[]{:S(2)}) collective-permute-start(f32[168,384]{1,0:T(8,128)S(1)} %get-tuple-element.36), channel_id=1, source_target_pairs={{1,2},{2,1},{3,4},{4,3},{5,6},{6,5},{7,8},{8,7},{9,10},{10,9},{11,... | collective-permute-start | bytes 774152 | tf_op jit(solution)/shard_map/ppermute | solution.py:441
  18.4 16.0 %collective-permute-start.4 = (f32[168,256]{1,0:T(8,128)S(1)}, f32[168,256]{1,0:T(8,128)S(1)}, u32[]{:S(2)}, u32[]{:S(2)}) collective-permute-start(f32[168,256]{1,0:T(8,128)S(1)} %get-tuple-element.40), channel_id=1, source_target_pairs={{0,1},{1,0},{2,3},{3,2},{4,5},{5,4},{6,7},{7,6},{8,9},{9,8},{10,11... | collective-permute-start | bytes 516104 | tf_op jit(solution)/shard_map/ppermute | solution.py:442
  20.7 13.7 %collective-permute-start.5 = (f32[168,256]{1,0:T(8,128)S(1)}, f32[168,256]{1,0:T(8,128)S(1)}, u32[]{:S(2)}, u32[]{:S(2)}) collective-permute-start(f32[168,256]{1,0:T(8,128)S(1)} %get-tuple-element.41), channel_id=1, source_target_pairs={{1,2},{2,1},{3,4},{4,3},{5,6},{6,5},{7,8},{8,7},{9,10},{10,9},{11,... | collective-permute-start | bytes 516104 | tf_op jit(solution)/shard_map/ppermute | solution.py:441
where the time goes:
time: 36.7 us; the launch traced here: 36.5 us
  blocking collectives  12.2 us (33%)
  Pallas kernels  9.77 us (27%)
  starting transfers between devices  9.01 us (25%)
  waiting for transfers between devices  4.85 us (13%)
  between operations  0.69 us (2%)
    all_to_all x1, blocking collectives, shards(): gathered = lax.all_to_all(dots, 'space', 0, 0, tiled=True)  12.2 us
    ppermute x3, starting transfers between devices, exchange(): got_far = lax.ppermute(far, ('grp', 'space'), outer)  5.53 us
    ppermute x3, waiting for transfers between devices, exchange(): got_far = lax.ppermute(far, ('grp', 'space'), outer)  4.84 us
    pallas_call x1, Pallas kernels, shards(): pl.pallas_call(build_kernel, out_shape=(weights, weights, wide, wide, wid...  3.74 us
    ppermute x3, starting transfers between devices, exchange(): got_near = lax.ppermute(near, 'space', inner)  3.48 us
    pallas_call x1, Pallas kernels, shards(): pl.pallas_call(functools.partial(final_kernel, peers), out_shape=(shape((...  2.11 us
    pallas_call x1, Pallas kernels, shards(): pl.pallas_call(functools.partial(second_kernel, peers), out_shape=(wide,...  1.77 us
    pallas_call x1, Pallas kernels, shards(): pl.pallas_call(send_kernel, out_shape=(wide, piece, piece), in_specs=hbm(...  1.18 us
  transfers between devices with their start and end apart: 6, of which 1 were waited for; matrix products, arithmetic and copies ran while one was open for 0% of the time, Pallas kernels for 10%

commit v1 on v0

--- a/solution.py
+++ b/solution.py
@@ -72,6 +72,38 @@
         for k, other, square in mine:
             total = total + scaled[k, square] * source[other * 8 : other * 8 + 8, :]
         target[term * 8 : term * 8 + 8, :] = total
+
+
+def packed_rows(tall):
+    return tall + pack_fold(tall)
+
+
+def pack_fold(tall):
+    return (tall // 2 + 7) // 8 * 8
+
+
+def pack(value, upper):
+    tall = value.shape[0]
+    fold = pack_fold(tall)
+    middle = value[:, LANES : 2 * LANES]
+    head, tail = middle[:fold], pltpu.roll(middle[tall - fold :], LANES // 2, 1)
+    low = lower_half(head)
+    whole = value[:, 2 * LANES :] if upper else value[:, :LANES]
+    return jnp.concatenate([whole, jnp.where(low, tail, head) if upper else jnp.where(low, head, tail)], axis=0)
+
+
+def unpack(lower, upper):
+    tall = lower.shape[0] * 2 // 3 // 8 * 8
+    while packed_rows(tall) > lower.shape[0]:
+        tall -= 8
+    fold = pack_fold(tall)
+
+    def middle(got):
+        bent = got[tall:]
+        return jnp.concatenate([bent, pltpu.roll(bent, LANES // 2, 1)[2 * fold - tall :]], axis=0)
+
+    first, second = middle(lower), middle(upper)
+    return jnp.concatenate([lower[:tall], jnp.where(lower_half(first), first, second), upper[:tall]], axis=1)
 
 
 def spread_rows(target, chunk, value):
@@ -183,7 +215,7 @@
         field_p[0:terms, lanes] = permute_blocks(field, order, chunk, terms)
         field_p[terms:tall, lanes] = jnp.zeros((tall - terms, LANES), F32)
     value = field_p[...]
-    store_sides(near, far, value[:, : nodes - LANES], value[:, LANES:])
+    store_sides(near, far, pack(value, False), pack(value, True))
 
 
 def build_kernel(
@@ -198,16 +230,18 @@
     steps = flat // LANES
     chunks = nodes // LANES
     small = [
-        pltpu.make_async_copy(source, target, sems.at[blocks + i])
+        pltpu.make_async_copy(source, target, sems.at[slots // 8 + i])
         for i, (source, target) in enumerate(
             ((sends_in, sends), (cols_in, cols), (cap_in, cap.at[0]), (var_in, var))
         )
     ]
     for copy in small:
         copy.start()
-    copies = [pltpu.make_async_copy(base.at[j], buf.at[j], sems.at[j]) for j in range(blocks)]
-    for copy in copies:
-        copy.start()
+    copies = []
+    for i in range(slots // 8):
+        some = (slice(None), pl.ds(8 * i, 8))
+        copies.append(pltpu.make_async_copy(base.at[some], buf.at[some], sems.at[i]))
+        copies[-1].start()
     for copy in small:
         copy.wait()
     order = order_of(sends)
@@ -230,9 +264,8 @@
 
     for one in acc:
         one[...] = jnp.zeros_like(one)
-    for copy in copies:
-        copy.wait()
     for slot in range(0, slots, 8):
+        copies[slot // 8].wait()
         for j in range(blocks):
             spots = [j if s == 0 else place[cols[order[j], s - 1]] for s in range(slot, slot + 8)]
             for step in range(0, steps, 8):
@@ -279,12 +312,10 @@
     w_high, w_low, field, part, near_own, flux_halo, coef_halo, got_near, got_far,
     local, halo_flux, near, far, major, result,
 ):
-    tall, nodes = field.shape
+    _, nodes = field.shape
     terms = len(chaos_links())
     below, above = by_side(got_near[...], got_far[...])
-    gap = jnp.zeros((tall, LANES), F32)
-    halo = jnp.concatenate([below, gap], axis=1)
-    halo = jnp.where(lower_half(halo), halo, jnp.concatenate([gap, above], axis=1))
+    halo = unpack(below, above)
     value = field[...]
     row = row_iota(value.shape)
     mixed = near_own[...] + product(
@@ -341,7 +372,7 @@
     outer = outer - flux[:, nodes:]
     outer = jnp.where(row < terms, outer, 0.0)
     local2[...] = own
-    store_sides(near, far, outer[:, LANES:], outer[:, : nodes - LANES])
+    store_sides(near, far, pack(outer, True), pack(outer, False))
     sums = [
         lane_dot(field[...], field[...]),
         lane_dot(field[...], value),
@@ -363,7 +394,6 @@
     solution_out, residual_out, place, work, out, sems,
 ):
     terms, nodes = solution_out.shape
-    tall = field.shape[0]
     order = order_of(sends)
     blocks = len(order)
     for j in range(blocks):
@@ -399,9 +429,7 @@
     work[0] = c1 * field[...] - c2 * image[...]
     put(0, solution_out)
     below, above = by_side(got_near[...], got_far[...])
-    gap = jnp.zeros((tall, LANES), F32)
-    inward = jnp.concatenate([above, gap], axis=1)
-    inward = jnp.where(lower_half(inward), inward, jnp.concatenate([gap, below], axis=1))
+    inward = unpack(above, below)
     work[1] = field[...] - c1 * image[...] + c2 * (local2[...] + inward)
     put(1, residual_out)
     for copy in copies:
@@ -451,7 +479,7 @@
     steps = flat // LANES
     params = pltpu.CompilerParams(vmem_limit_bytes=48 * 1024 * 1024)
     wide = shape((tall, nodes))
-    piece = shape((tall, nodes - LANES))
+    piece = shape((packed_rows(tall), LANES))
     coefs = shape((8 * (VARS + 1), LANES))
     weights = shape((nodes, 2 * nodes), BF16)
     spread = pltpu.VMEM((tall * 8, LANES), F32)
@@ -489,7 +517,7 @@
             pltpu.VMEM((1, nodes), F32),
             pltpu.VMEM((VARS, nodes), F32),
             pltpu.SMEM((2 * blocks,), jnp.int32),
-            pltpu.SemaphoreType.DMA((blocks + 4,)),
+            pltpu.SemaphoreType.DMA((slots // 8 + 4,)),
         ],
         compiler_params=params,
         cost_estimate=pl.CostEstimate(flops=10**9, bytes_accessed=4 * 10**6, transcendentals=0),

time: 36.7 us -> 35.9 us (0.978)
  starting transfers between devices: 9.01 us -> 8.48 us
    ppermute x3, starting transfers between devices: 3.48 us -> 2.85 us  [exchange(): got_near = lax.ppermute(near, 'space', inner)]
    pallas_call x1, Pallas kernels: 3.74 us -> 3.36 us  [shards(): pl.pallas_call(build_kernel, out_shape=(weights, weights, wide, wide, wid...]
  transfers between devices with their start and end apart: 6 -> 6, of which waited for: 1 -> 1; matrix products, arithmetic and copies ran while one was open for 0% -> 0% of each run, Pallas kernels for 10% -> 9%
where the time goes in v1:
time: 35.9 us; the launch traced here: 35.7 us
  blocking collectives  12.3 us (34%)
  Pallas kernels  9.41 us (26%)
  starting transfers between devices  8.48 us (24%)
  waiting for transfers between devices  4.75 us (13%)
  between operations  0.69 us (2%)
    all_to_all x1, blocking collectives, shards(): gathered = lax.all_to_all(dots, 'space', 0, 0, tiled=True)  12.3 us
    ppermute x3, starting transfers between devices, exchange(): got_far = lax.ppermute(far, ('grp', 'space'), outer)  5.63 us
    ppermute x3, waiting for transfers between devices, exchange(): got_far = lax.ppermute(far, ('grp', 'space'), outer)  4.74 us
    pallas_call x1, Pallas kernels, shards(): pl.pallas_call(build_kernel, out_shape=(weights, weights, wide, wide, wid...  3.36 us
    ppermute x3, starting transfers between devices, exchange(): got_near = lax.ppermute(near, 'space', inner)  2.85 us
    pallas_call x1, Pallas kernels, shards(): pl.pallas_call(functools.partial(final_kernel, peers), out_shape=(shape((...  2.09 us
    pallas_call x1, Pallas kernels, shards(): pl.pallas_call(functools.partial(second_kernel, peers), out_shape=(wide,...  1.78 us
    pallas_call x1, Pallas kernels, shards(): pl.pallas_call(send_kernel, out_shape=(wide, piece, piece), in_specs=hbm(...  1.2 us
  transfers between devices with their start and end apart: 6, of which 1 were waited for; matrix products, arithmetic and copies ran while one was open for 0% of the time, Pallas kernels for 9%

profile of v1, /device:TPU:0, one launch (start us, length us, event | category | flops | bytes accessed | tf_op | source)
XLA Modules:
  0.0 35.7 jit_solution(2504715851815048837)
XLA Ops:
  0.6 1.2 %send.1 = (f32[168,384]{1,0:T(8,128)S(1)}, f32[256,128]{1,0:T(8,128)S(1)}, f32[256,128]{1,0:T(8,128)S(1)}) custom-call(s32[1,2,3]{2,1,0:T(2,128)} %sends.1, f32[165,384]{1,0:T(8,128)} %field_in.1), custom_call_target="tpu_custom_call" | custom-call | tf_op jit(solution)/shard_map/send/pallas_call | solution.py:488
  1.8 0.6 %collective-permute-start = (f32[256,128]{1,0:T(8,128)S(1)}, f32[256,128]{1,0:T(8,128)S(1)}, u32[]{:S(2)}, u32[]{:S(2)}) collective-permute-start(f32[256,128]{1,0:T(8,128)S(1)} %get-tuple-element.29), channel_id=1, source_target_pairs={{0,1},{1,0},{2,3},{3,2},{4,5},{5,4},{6,7},{7,6},{8,9},{9,8},{10,11... | collective-permute-start | bytes 393224 | tf_op jit(solution)/shard_map/ppermute | solution.py:470
  2.4 2.6 %collective-permute-start.1 = (f32[256,128]{1,0:T(8,128)S(1)}, f32[256,128]{1,0:T(8,128)S(1)}, u32[]{:S(2)}, u32[]{:S(2)}) collective-permute-start(f32[256,128]{1,0:T(8,128)S(1)} %get-tuple-element.30), channel_id=1, source_target_pairs={{1,2},{2,1},{3,4},{4,3},{5,6},{6,5},{7,8},{8,7},{9,10},{10,9},{11,... | collective-permute-start | bytes 393224 | tf_op jit(solution)/shard_map/ppermute | solution.py:469
  4.9 3.4 %build.1 = (bf16[384,768]{1,0:T(8,128)(2,1)S(1)}, bf16[384,768]{1,0:T(8,128)(2,1)S(1)}, f32[168,384]{1,0:T(8,128)S(1)}, f32[168,384]{1,0:T(8,128)S(1)}, f32[168,...) custom-call(s32[1,2,3]{2,1,0:T(2,128)} %sends.1, s32[6,23]{1,0:T(8,128)} %cols_in.1, ...), custom_call_target="tpu_custom_call" | custom-call | flops 1000000000 | bytes 4000000 | tf_op jit(solution)/shard_map/build/pallas_call | solution.py:503
  8.3 0.0 collective-permute-done.got_near
  8.3 0.0 collective-permute-done.1.got_far
  8.3 0.0 copy-start
  8.3 1.0 %local.1 = (f32[168,384]{1,0:T(8,128)S(1)}, f32[168,384]{1,0:T(8,128)S(1)}, f32[168,384]{1,0:T(8,128)S(1)}, f32[168,384]{1,0:T(8,128)S(1)}) custom-call(bf16[384,768]{1,0:T(8,128)(2,1)S(1)} %get-tuple-element.23.w_high, bf16[384,768]{1,0:T(8,128)(2,1)S(1)} %get-tuple-element.24.w_low, f32[168,384]{1,0:T(8,128)S(1)} %get-tuple-element.22.field_p.field, ...), custom_call_target="tpu_custom_call" | custom-call | tf_op jit(solution)/shard_map/local/pallas_call | solution.py:527
  9.3 0.2 collective-permute-start.2
  9.5 1.6 %collective-permute-start.3 = (f32[168,384]{1,0:T(8,128)S(1)}, f32[168,384]{1,0:T(8,128)S(1)}, u32[]{:S(2)}, u32[]{:S(2)}) collective-permute-start(f32[168,384]{1,0:T(8,128)S(1)} %get-tuple-element.36), channel_id=1, source_target_pairs={{1,2},{2,1},{3,4},{4,3},{5,6},{6,5},{7,8},{8,7},{9,10},{10,9},{11,... | collective-permute-start | bytes 774152 | tf_op jit(solution)/shard_map/ppermute | solution.py:469
  11.1 0.0 collective-permute-done.2.got_near
  11.1 4.7 %collective-permute-done.3.got_far = f32[168,384]{1,0:T(8,128)S(1)} collective-permute-done((f32[168,384]{1,0:T(8,128)S(1)}, f32[168,384]{1,0:T(8,128)S(1)}, u32[]{:S(2)}, u32[]{:S(2)}) %collective-permute-start.3) | collective-permute-done | bytes 258080 | tf_op jit(solution)/shard_map/ppermute | solution.py:469
  15.8 1.8 %second.1 = (f32[168,384]{1,0:T(8,128)S(1)}, f32[168,384]{1,0:T(8,128)S(1)}, f32[256,128]{1,0:T(8,128)S(1)}, f32[256,128]{1,0:T(8,128)S(1)}, f32[16,1,128]{2,1,0:T(1,128)S(1)}) custom-call(bf16[384,768]{1,0:T(8,128)(2,1)S(1)} %get-tuple-element.23.w_high, bf16[384,768]{1,0:T(8,128)(2,1)S(1)} %get-tuple-element.24.w_low, ...), custom_call_target="tpu_custom_call" | custom-call | tf_op jit(solution)/shard_map/second/pallas_call | solution.py:538
  17.6 2.1 %collective-permute-start.4 = (f32[256,128]{1,0:T(8,128)S(1)}, f32[256,128]{1,0:T(8,128)S(1)}, u32[]{:S(2)}, u32[]{:S(2)}) collective-permute-start(f32[256,128]{1,0:T(8,128)S(1)} %get-tuple-element.40), channel_id=1, source_target_pairs={{0,1},{1,0},{2,3},{3,2},{4,5},{5,4},{6,7},{7,6},{8,9},{9,8},{10,11... | collective-permute-start | bytes 393224 | tf_op jit(solution)/shard_map/ppermute | solution.py:470
  19.7 1.5 %collective-permute-start.5 = (f32[256,128]{1,0:T(8,128)S(1)}, f32[256,128]{1,0:T(8,128)S(1)}, u32[]{:S(2)}, u32[]{:S(2)}) collective-permute-start(f32[256,128]{1,0:T(8,128)S(1)} %get-tuple-element.41), channel_id=1, source_target_pairs={{1,2},{2,1},{3,4},{4,3},{5,6},{6,5},{7,8},{8,7},{9,10},{10,9},{11,... | collective-permute-start | bytes 393224 | tf_op jit(solution)/shard_map/ppermute | solution.py:469
  21.2 12.3 %all_to_all.5.dots = f32[16,1,128]{2,1,0:T(1,128)S(1)} all-to-all(f32[16,1,128]{2,1,0:T(1,128)S(1)} %get-tuple-element.37), channel_id=1, replica_groups=mesh['grp'=2,'space'=16] {'space'}, dimensions={0} | all-to-all | bytes 16384 | tf_op jit(solution)/shard_map/all_to_all | solution.py:548
  33.6 0.0 collective-permute-done.4.got_near
  33.6 0.0 collective-permute-done.5.got_far
  33.6 0.0 copy-done
  33.6 2.1 %finish.1 = (f32[165,384]{1,0:T(8,128)}, f32[165,384]{1,0:T(8,128)}) custom-call(s32[1,2,3]{2,1,0:T(2,128)S(1)} %copy-done, f32[16,1,128]{2,1,0:T(1,128)S(1)} %all_to_all.5.dots, f32[168,384]{1,0:T(8,128)S(1)} %get-tuple-element.22.field_p.field, f32[168,384]{1,0:T(8,128)S(1)} %get-tuple-element.38.image, f32[168,384]{1,0:T(8,128)S(1)} %get-tuple-element.39.local2, ...), custom_call_target="tpu_custom_call" | custom-call | tf_op jit(solution)/shard_map/finish/pallas_call | solution.py:550
Async XLA Ops:
  1.8 6.5 %collective-permute-start = (f32[256,128]{1,0:T(8,128)S(1)}, f32[256,128]{1,0:T(8,128)S(1)}, u32[]{:S(2)}, u32[]{:S(2)}) collective-permute-start(f32[256,128]{1,0:T(8,128)S(1)} %get-tuple-element.29), channel_id=1, source_target_pairs={{0,1},{1,0},{2,3},{3,2},{4,5},{5,4},{6,7},{7,6},{8,9},{9,8},{10,11... | collective-permute-start | bytes 393224 | tf_op jit(solution)/shard_map/ppermute | solution.py:470
  2.4 5.9 %collective-permute-start.1 = (f32[256,128]{1,0:T(8,128)S(1)}, f32[256,128]{1,0:T(8,128)S(1)}, u32[]{:S(2)}, u32[]{:S(2)}) collective-permute-start(f32[256,128]{1,0:T(8,128)S(1)} %get-tuple-element.30), channel_id=1, source_target_pairs={{1,2},{2,1},{3,4},{4,3},{5,6},{6,5},{7,8},{8,7},{9,10},{10,9},{11,... | collective-permute-start | bytes 393224 | tf_op jit(solution)/shard_map/ppermute | solution.py:469
  8.3 25.2 %copy-start = (s32[1,2,3]{2,1,0:T(2,128)S(1)}, s32[1,2,3]{2,1,0:T(2,128)}, u32[]{:S(2)}) copy-start(s32[1,2,3]{2,1,0:T(2,128)} %sends.1) | copy-start | bytes 76
  9.3 1.8 %collective-permute-start.2 = (f32[168,384]{1,0:T(8,128)S(1)}, f32[168,384]{1,0:T(8,128)S(1)}, u32[]{:S(2)}, u32[]{:S(2)}) collective-permute-start(f32[168,384]{1,0:T(8,128)S(1)} %get-tuple-element.35), channel_id=1, source_target_pairs={{0,1},{1,0},{2,3},{3,2},{4,5},{5,4},{6,7},{7,6},{8,9},{9,8},{10,11... | collective-permute-start | bytes 774152 | tf_op jit(solution)/shard_map/ppermute | solution.py:470
  9.5 6.3 %collective-permute-start.3 = (f32[168,384]{1,0:T(8,128)S(1)}, f32[168,384]{1,0:T(8,128)S(1)}, u32[]{:S(2)}, u32[]{:S(2)}) collective-permute-start(f32[168,384]{1,0:T(8,128)S(1)} %get-tuple-element.36), channel_id=1, source_target_pairs={{1,2},{2,1},{3,4},{4,3},{5,6},{6,5},{7,8},{8,7},{9,10},{10,9},{11,... | collective-permute-start | bytes 774152 | tf_op jit(solution)/shard_map/ppermute | solution.py:469
  17.6 16.0 %collective-permute-start.4 = (f32[256,128]{1,0:T(8,128)S(1)}, f32[256,128]{1,0:T(8,128)S(1)}, u32[]{:S(2)}, u32[]{:S(2)}) collective-permute-start(f32[256,128]{1,0:T(8,128)S(1)} %get-tuple-element.40), channel_id=1, source_target_pairs={{0,1},{1,0},{2,3},{3,2},{4,5},{5,4},{6,7},{7,6},{8,9},{9,8},{10,11... | collective-permute-start | bytes 393224 | tf_op jit(solution)/shard_map/ppermute | solution.py:470
  19.7 13.8 %collective-permute-start.5 = (f32[256,128]{1,0:T(8,128)S(1)}, f32[256,128]{1,0:T(8,128)S(1)}, u32[]{:S(2)}, u32[]{:S(2)}) collective-permute-start(f32[256,128]{1,0:T(8,128)S(1)} %get-tuple-element.41), channel_id=1, source_target_pairs={{1,2},{2,1},{3,4},{4,3},{5,6},{6,5},{7,8},{8,7},{9,10},{10,9},{11,... | collective-permute-start | bytes 393224 | tf_op jit(solution)/shard_map/ppermute | solution.py:469

commit v2 on v1

--- a/solution.py
+++ b/solution.py
@@ -220,7 +220,7 @@
 
 def build_kernel(
     sends_in, cols_in, cap_in, var_in, base, field_p,
-    w_high, w_low, part, near_own, flux_out, coef_own, coef_halo, cap_p,
+    w_high, w_low, flux_own, outer_out, near, far, coef_own, coef_halo, cap_p,
     buf, acc, dense, major, result, weights_p, sends, cols, cap, var, place, sems,
 ):
     blocks, slots, flat = base.shape
@@ -275,15 +275,15 @@
                 for spot, tile in zip(spots, transpose8(tiles)):
                     acc[j][spot, step : step + 8, :] += tile
     row = row_iota((8, LANES))
-    near = lane_iota((8, LANES)) < width
+    nigh = lane_iota((8, LANES)) < width
     for j in range(blocks):
         for pair in range(blocks):
             lanes = slice(pair * LANES, (pair + 1) * LANES)
             for step in range(0, steps, 8):
                 even = acc[j][2 * pair, step : step + 8, :]
                 odd = acc[j][2 * pair + 1, step : step + 8, :]
-                first = jnp.where(near, even, pltpu.roll(odd, width, 1))
-                second = jnp.where(near, pltpu.roll(even, width, 1), odd)
+                first = jnp.where(nigh, even, pltpu.roll(odd, width, 1))
+                second = jnp.where(nigh, pltpu.roll(even, width, 1), odd)
                 for half in range(2):
                     pick = row // 2 + 4 * half
                     start = j * width + 2 * step + 8 * half
@@ -300,50 +300,58 @@
     flux = product(*split(left), w_high[...], w_low[...], ((1,), (0,)))
     for coef, first, lanes in ((coef_own, chunks, slice(0, nodes)), (coef_halo, chunks, slice(nodes, 2 * nodes))):
         set_coefs(coef, first, flux[terms : terms + 1, lanes], flux[tall : tall + VARS, lanes])
-    flux_out[...] = flux[0:tall, nodes:]
-    near_own[...] = product(
-        *split(marked(value, terms)), w_high[:, 0:nodes], w_low[:, 0:nodes], ((1,), (1,))
-    )
+    flux_own[...] = flux[0:tall, 0:nodes]
+    outer = flux[:, nodes:]
+    outer_out[...] = outer
+    store_sides(near, far, pack(outer, True), pack(outer, False))
+
+
+def local_kernel(
+    w_high, w_low, field, flux_own, cap, coef_own, got_near, got_far,
+    local, halo_out, near, far, major, result,
+):
+    terms = len(chaos_links())
+    halo = unpack(*by_side(got_near[...], got_far[...]))
+    halo_out[...] = halo
+    value = field[...]
+    row = row_iota(value.shape)
+    extended = split(marked(jnp.concatenate([value, halo], axis=1), terms))
+    mixed = product(*extended, w_high[...], w_low[...], ((1,), (1,)))
+    to_terms(major, mixed[terms : terms + 1, :] * value - mixed, value)
     couple(major, result, coef_list(coef_own))
-    part[...] = cap_p[...] * value + from_terms(result, 2)[1] - flux[0:tall, 0:nodes]
-
-
-def local_kernel(
-    w_high, w_low, field, part, near_own, flux_halo, coef_halo, got_near, got_far,
-    local, halo_flux, near, far, major, result,
-):
-    _, nodes = field.shape
+    forward, transferred = from_terms(result, 2)
+    own = jnp.where(row < terms, cap[...] * value + forward + transferred - flux_own[...], 0.0)
+    local[...] = own
+    store_sides(near, far, pack(own, False), pack(own, True))
+
+
+def flux_kernel(field, halo, outer, got_near, got_far, inward, outward, coef, major, result):
+    tall, nodes = field.shape
     terms = len(chaos_links())
     below, above = by_side(got_near[...], got_far[...])
-    halo = unpack(below, above)
-    value = field[...]
-    row = row_iota(value.shape)
-    mixed = near_own[...] + product(
-        *split(marked(halo, terms)), w_high[:, nodes:], w_low[:, nodes:], ((1,), (1,))
-    )
-    to_terms(major, mixed[terms : terms + 1, :] * value - mixed, halo)
-    couple(major, result, coef_list(coef_halo))
-    forward, outer = from_terms(result, 2)
-    own = jnp.where(row < terms, part[...] + forward, 0.0)
-    outer = jnp.where(row < terms, outer - flux_halo[...], 0.0)
-    local[...] = own
-    halo_flux[...] = outer
-    half = lower_half(own)
-    store_sides(near, far, jnp.where(half, own, outer), jnp.where(half, outer, own))
+    inflow = unpack(above, below)
+    outer = outer[...]
+    coef[...] = jnp.zeros_like(coef)
+    for first, flux in ((0, inflow), (nodes // LANES, outer)):
+        set_coefs(coef, first, flux[terms : terms + 1, :], flux[tall : tall + VARS, :])
+    to_terms(major, field[...], halo[...])
+    couple(major, result, coef_list(coef))
+    own, other = from_terms(result, 2)
+    row = row_iota(own.shape)
+    inward[...] = jnp.where(row < terms, own - inflow[0:tall], 0.0)
+    outward[...] = jnp.where(row < terms, other - outer[0:tall], 0.0)
 
 
 def second_kernel(
     peers,
-    w_high, w_low, field, local, halo_flux, cap, coef_own, coef_halo, got_near, got_far,
+    w_high, w_low, field, local, inward, outward, cap, coef_own, coef_halo, got_near, got_far,
     image, local2, near, far, dots, major, result, major2, result2,
 ):
     _, nodes = field.shape
     terms = len(chaos_links())
-    below, above = by_side(got_near[...], got_far[...])
-    half = lower_half(below)
-    row = row_iota(below.shape)
-    value = jnp.where(row < terms, local[...] + jnp.where(half, above, below), 0.0)
-    halo = jnp.where(row < terms, halo_flux[...] + jnp.where(half, below, above), 0.0)
+    value = local[...] + inward[...]
+    halo = unpack(*by_side(got_near[...], got_far[...])) + outward[...]
+    row = row_iota(value.shape)
     image[...] = value
     to_terms(major, value, value)
     extended = split(marked(jnp.concatenate([value, halo], axis=1), terms))
@@ -500,11 +508,13 @@
     )(sends, in_hbm(right_side))
     got = exchange(near, far)
 
-    w_high, w_low, part, near_own, flux_halo, coef_own, coef_halo, cap = pl.pallas_call(
+    tallest = shape((tall + VARS, nodes))
+    deep = shape((packed_rows(tall + VARS), LANES))
+    w_high, w_low, flux_own, outer, near, far, coef_own, coef_halo, cap = pl.pallas_call(
         build_kernel,
-        out_shape=(weights, weights, wide, wide, wide, coefs, coefs, shape((1, nodes))),
+        out_shape=(weights, weights, wide, tallest, deep, deep, coefs, coefs, shape((1, nodes))),
         in_specs=hbm(5) + vmem(1),
-        out_specs=tuple(vmem(8)),
+        out_specs=tuple(vmem(9)),
         scratch_shapes=[
             pltpu.VMEM((blocks, slots, flat), F32),
             [pltpu.VMEM((2 * blocks, steps, LANES), F32) for _ in range(blocks)],
@@ -524,26 +534,37 @@
         name="build",
     )(sends, in_hbm(block_cols), in_hbm(capacity), in_hbm(var_field), in_hbm(base_cond), field)
 
-    local, halo_flux, near, far = pl.pallas_call(
+    got_flux = exchange(near, far)
+
+    local, halo, near, far = pl.pallas_call(
         local_kernel,
-        out_shape=(wide, wide, wide, wide),
-        in_specs=vmem(9),
+        out_shape=(wide, wide, piece, piece),
+        in_specs=vmem(8),
         out_specs=tuple(vmem(4)),
         scratch_shapes=[spread] * 2,
         compiler_params=params,
         name="local",
-    )(w_high, w_low, field, part, near_own, flux_halo, coef_halo, *got)
+    )(w_high, w_low, field, flux_own, cap, coef_own, *got)
     got = exchange(near, far)
+    inward, outward = pl.pallas_call(
+        flux_kernel,
+        out_shape=(wide, wide),
+        in_specs=vmem(5),
+        out_specs=tuple(vmem(2)),
+        scratch_shapes=[pltpu.VMEM(coefs.shape, F32)] + [spread] * 2,
+        compiler_params=params,
+        name="flux",
+    )(field, halo, outer, *got_flux)
 
     image, local2, near, far, dots = pl.pallas_call(
         functools.partial(second_kernel, peers),
         out_shape=(wide, wide, piece, piece, shape((peers, 1, LANES))),
-        in_specs=vmem(10),
+        in_specs=vmem(11),
         out_specs=tuple(vmem(5)),
         scratch_shapes=[spread] * 4,
         compiler_params=params,
         name="second",
-    )(w_high, w_low, field, local, halo_flux, cap, coef_own, coef_halo, *got)
+    )(w_high, w_low, field, local, inward, outward, cap, coef_own, coef_halo, *got)
     got = exchange(near, far)
     gathered = lax.all_to_all(dots, "space", 0, 0, tiled=True)
 

time: 35.9 us -> 33.6 us (0.936)
  waiting for transfers between devices: 4.75 us -> 3.02 us
  starting transfers between devices: 8.48 us -> 8.07 us
    ppermute x3 -> x4, starting transfers between devices: 2.85 us -> 1.07 us  [exchange(): got_near = lax.ppermute(near, 'space', inner)]
    ppermute x3 -> x4, waiting for transfers between devices: 4.74 us -> 3.01 us  [exchange(): got_far = lax.ppermute(far, ('grp', 'space'), outer)]
    ppermute x3 -> x4, starting transfers between devices: 5.63 us -> 7 us  [exchange(): got_far = lax.ppermute(far, ('grp', 'space'), outer)]
    pallas_call x2 -> x3, Pallas kernels: 4.35 us -> 4.51 us  [the longest x1 2.95 us: shards(): pl.pallas_call(build_kernel, out_shape=(weights, weights, wide, tallest,...]
  transfers between devices with their start and end apart: 6 -> 8, of which waited for: 1 -> 2; matrix products, arithmetic and copies ran while one was open for 0% -> 0% of each run, Pallas kernels for 9% -> 14%
where the time goes in v2:
time: 33.6 us; the launch traced here: 33.4 us
  blocking collectives  12.1 us (36%)
  Pallas kernels  9.54 us (28%)
  starting transfers between devices  8.07 us (24%)
  waiting for transfers between devices  3.02 us (9%)
  between operations  0.68 us (2%)
    all_to_all x1, blocking collectives, shards(): gathered = lax.all_to_all(dots, 'space', 0, 0, tiled=True)  12.1 us
    ppermute x4, starting transfers between devices, exchange(): got_far = lax.ppermute(far, ('grp', 'space'), outer)  7 us
    ppermute x4, waiting for transfers between devices, exchange(): got_far = lax.ppermute(far, ('grp', 'space'), outer)  3.01 us
    pallas_call x1, Pallas kernels, shards(): pl.pallas_call(build_kernel, out_shape=(weights, weights, wide, tallest,...  2.95 us
    pallas_call x1, Pallas kernels, shards(): pl.pallas_call(functools.partial(final_kernel, peers), out_shape=(shape((...  2.08 us
    pallas_call x1, Pallas kernels, shards(): pl.pallas_call(functools.partial(second_kernel, peers), out_shape=(wide,...  1.74 us
    pallas_call x1, Pallas kernels, shards(): pl.pallas_call(send_kernel, out_shape=(wide, piece, piece), in_specs=hbm(...  1.2 us
    pallas_call x1, Pallas kernels, shards(): pl.pallas_call(local_kernel, out_shape=(wide, wide, piece, piece), in_spe...  1.08 us
  transfers between devices with their start and end apart: 8, of which 2 were waited for; matrix products, arithmetic and copies ran while one was open for 0% of the time, Pallas kernels for 14%

profile of v2, /device:TPU:0, one launch (start us, length us, event | category | flops | bytes accessed | tf_op | source)
XLA Modules:
  0.0 33.4 jit_solution(3720272481039349845)
XLA Ops:
  0.6 1.2 %send.1 = (f32[168,384]{1,0:T(8,128)S(1)}, f32[256,128]{1,0:T(8,128)S(1)}, f32[256,128]{1,0:T(8,128)S(1)}) custom-call(s32[1,2,3]{2,1,0:T(2,128)} %sends.1, f32[165,384]{1,0:T(8,128)} %field_in.1), custom_call_target="tpu_custom_call" | custom-call | tf_op jit(solution)/shard_map/send/pallas_call | solution.py:496
  1.8 0.6 %collective-permute-start = (f32[256,128]{1,0:T(8,128)S(1)}, f32[256,128]{1,0:T(8,128)S(1)}, u32[]{:S(2)}, u32[]{:S(2)}) collective-permute-start(f32[256,128]{1,0:T(8,128)S(1)} %get-tuple-element.31), channel_id=1, source_target_pairs={{0,1},{1,0},{2,3},{3,2},{4,5},{5,4},{6,7},{7,6},{8,9},{9,8},{10,11... | collective-permute-start | bytes 393224 | tf_op jit(solution)/shard_map/ppermute | solution.py:478
  2.4 2.6 %collective-permute-start.1 = (f32[256,128]{1,0:T(8,128)S(1)}, f32[256,128]{1,0:T(8,128)S(1)}, u32[]{:S(2)}, u32[]{:S(2)}) collective-permute-start(f32[256,128]{1,0:T(8,128)S(1)} %get-tuple-element.32), channel_id=1, source_target_pairs={{1,2},{2,1},{3,4},{4,3},{5,6},{6,5},{7,8},{8,7},{9,10},{10,9},{11,... | collective-permute-start | bytes 393224 | tf_op jit(solution)/shard_map/ppermute | solution.py:477
  4.9 2.9 %build.1 = (bf16[384,768]{1,0:T(8,128)(2,1)S(1)}, bf16[384,768]{1,0:T(8,128)(2,1)S(1)}, f32[168,384]{1,0:T(8,128)S(1)}, f32[176,384]{1,0:T(8,128)S(1)}, f32[264,...) custom-call(s32[1,2,3]{2,1,0:T(2,128)} %sends.1, ...), custom_call_target="tpu_custom_call" | custom-call | flops 1000000000 | bytes 4000000 | tf_op jit(solution)/shard_map/build/pallas_call | solution.py:513
  7.9 0.2 collective-permute-start.2
  8.1 1.5 %collective-permute-start.3 = (f32[264,128]{1,0:T(8,128)S(1)}, f32[264,128]{1,0:T(8,128)S(1)}, u32[]{:S(2)}, u32[]{:S(2)}) collective-permute-start(f32[264,128]{1,0:T(8,128)S(1)} %get-tuple-element.37), channel_id=1, source_target_pairs={{1,2},{2,1},{3,4},{4,3},{5,6},{6,5},{7,8},{8,7},{9,10},{10,9},{11,... | collective-permute-start | bytes 405512 | tf_op jit(solution)/shard_map/ppermute | solution.py:477
  9.6 0.0 collective-permute-done.got_near
  9.6 0.0 collective-permute-done.1.got_far
  9.6 1.1 %local.1 = (f32[168,384]{1,0:T(8,128)S(1)}, f32[168,384]{1,0:T(8,128)S(1)}, f32[256,128]{1,0:T(8,128)S(1)}, f32[256,128]{1,0:T(8,128)S(1)}) custom-call(bf16[384,768]{1,0:T(8,128)(2,1)S(1)} %get-tuple-element.26.w_high, bf16[384,768]{1,0:T(8,128)(2,1)S(1)} %get-tuple-element.27.w_low, f32[168,384]{1,0:T(8,128)S(1)} %get-tuple-element.25.field_p.field, ...), custom_call_target="tpu_custom_call" | custom-call | tf_op jit(solution)/shard_map/local/pallas_call | solution.py:539
  10.7 0.2 collective-permute-start.4
  10.9 1.5 %collective-permute-start.5 = (f32[256,128]{1,0:T(8,128)S(1)}, f32[256,128]{1,0:T(8,128)S(1)}, u32[]{:S(2)}, u32[]{:S(2)}) collective-permute-start(f32[256,128]{1,0:T(8,128)S(1)} %get-tuple-element.42), channel_id=1, source_target_pairs={{1,2},{2,1},{3,4},{4,3},{5,6},{6,5},{7,8},{8,7},{9,10},{10,9},{11,... | collective-permute-start | bytes 393224 | tf_op jit(solution)/shard_map/ppermute | solution.py:477
  12.4 0.0 collective-permute-done.2.got_near
  12.4 0.7 %collective-permute-done.3.got_far = f32[264,128]{1,0:T(8,128)S(1)} collective-permute-done((f32[264,128]{1,0:T(8,128)S(1)}, f32[264,128]{1,0:T(8,128)S(1)}, u32[]{:S(2)}, u32[]{:S(2)}) %collective-permute-start.3) | collective-permute-done | bytes 135200 | tf_op jit(solution)/shard_map/ppermute | solution.py:477
  13.1 0.5 %flux.1 = (f32[168,384]{1,0:T(8,128)S(1)}, f32[168,384]{1,0:T(8,128)S(1)}) custom-call(f32[168,384]{1,0:T(8,128)S(1)} %get-tuple-element.25.field_p.field, f32[168,384]{1,0:T(8,128)S(1)} %get-tuple-element.34.halo, f32[176,384]{1,0:T(8,128)S(1)} %get-tuple-element.35.outer, f32[264,128]{1,0:T(8,128)S(1)} %collective-permute-done.2.got_near, ...), custom_call_target="tpu_custom_call" | custom-call | tf_op jit(solution)/shard_map/flux/pallas_call | solution.py:549
  13.6 0.0 collective-permute-done.4.got_near
  13.6 2.3 %collective-permute-done.5.got_far = f32[256,128]{1,0:T(8,128)S(1)} collective-permute-done((f32[256,128]{1,0:T(8,128)S(1)}, f32[256,128]{1,0:T(8,128)S(1)}, u32[]{:S(2)}, u32[]{:S(2)}) %collective-permute-start.5) | collective-permute-done | bytes 131104 | tf_op jit(solution)/shard_map/ppermute | solution.py:477
  15.9 1.7 %second.1 = (f32[168,384]{1,0:T(8,128)S(1)}, f32[168,384]{1,0:T(8,128)S(1)}, f32[256,128]{1,0:T(8,128)S(1)}, f32[256,128]{1,0:T(8,128)S(1)}, f32[16,1,128]{2,1,0:T(1,128)S(1)}) custom-call(bf16[384,768]{1,0:T(8,128)(2,1)S(1)} %get-tuple-element.26.w_high, bf16[384,768]{1,0:T(8,128)(2,1)S(1)} %get-tuple-element.27.w_low, ...), custom_call_target="tpu_custom_call" | custom-call | tf_op jit(solution)/shard_map/second/pallas_call | solution.py:559
  17.6 0.1 collective-permute-start.6
  17.7 1.5 %collective-permute-start.7 = (f32[256,128]{1,0:T(8,128)S(1)}, f32[256,128]{1,0:T(8,128)S(1)}, u32[]{:S(2)}, u32[]{:S(2)}) collective-permute-start(f32[256,128]{1,0:T(8,128)S(1)} %get-tuple-element.47), channel_id=1, source_target_pairs={{1,2},{2,1},{3,4},{4,3},{5,6},{6,5},{7,8},{8,7},{9,10},{10,9},{11,... | collective-permute-start | bytes 393224 | tf_op jit(solution)/shard_map/ppermute | solution.py:477
  19.2 12.1 %all_to_all.5.dots = f32[16,1,128]{2,1,0:T(1,128)S(1)} all-to-all(f32[16,1,128]{2,1,0:T(1,128)S(1)} %get-tuple-element.43), channel_id=1, replica_groups=mesh['grp'=2,'space'=16] {'space'}, dimensions={0} | all-to-all | bytes 16384 | tf_op jit(solution)/shard_map/all_to_all | solution.py:569
  31.3 0.0 collective-permute-done.6.got_near
  31.3 0.0 collective-permute-done.7.got_far
  31.3 0.0 copy-done
  31.3 2.1 %finish.1 = (f32[165,384]{1,0:T(8,128)}, f32[165,384]{1,0:T(8,128)}) custom-call(s32[1,2,3]{2,1,0:T(2,128)S(1)} %copy-done, f32[16,1,128]{2,1,0:T(1,128)S(1)} %all_to_all.5.dots, f32[168,384]{1,0:T(8,128)S(1)} %get-tuple-element.25.field_p.field, f32[168,384]{1,0:T(8,128)S(1)} %get-tuple-element.44.image, f32[168,384]{1,0:T(8,128)S(1)} %get-tuple-element.45.local2, ...), custom_call_target="tpu_custom_call" | custom-call | tf_op jit(solution)/shard_map/finish/pallas_call | solution.py:571
  (1 shorter events, 0.0 us)
Async XLA Ops:
  1.8 7.8 %collective-permute-start = (f32[256,128]{1,0:T(8,128)S(1)}, f32[256,128]{1,0:T(8,128)S(1)}, u32[]{:S(2)}, u32[]{:S(2)}) collective-permute-start(f32[256,128]{1,0:T(8,128)S(1)} %get-tuple-element.31), channel_id=1, source_target_pairs={{0,1},{1,0},{2,3},{3,2},{4,5},{5,4},{6,7},{7,6},{8,9},{9,8},{10,11... | collective-permute-start | bytes 393224 | tf_op jit(solution)/shard_map/ppermute | solution.py:478
  2.4 7.2 %collective-permute-start.1 = (f32[256,128]{1,0:T(8,128)S(1)}, f32[256,128]{1,0:T(8,128)S(1)}, u32[]{:S(2)}, u32[]{:S(2)}) collective-permute-start(f32[256,128]{1,0:T(8,128)S(1)} %get-tuple-element.32), channel_id=1, source_target_pairs={{1,2},{2,1},{3,4},{4,3},{5,6},{6,5},{7,8},{8,7},{9,10},{10,9},{11,... | collective-permute-start | bytes 393224 | tf_op jit(solution)/shard_map/ppermute | solution.py:477
  7.9 4.5 %collective-permute-start.2 = (f32[264,128]{1,0:T(8,128)S(1)}, f32[264,128]{1,0:T(8,128)S(1)}, u32[]{:S(2)}, u32[]{:S(2)}) collective-permute-start(f32[264,128]{1,0:T(8,128)S(1)} %get-tuple-element.36), channel_id=1, source_target_pairs={{0,1},{1,0},{2,3},{3,2},{4,5},{5,4},{6,7},{7,6},{8,9},{9,8},{10,11... | collective-permute-start | bytes 405512 | tf_op jit(solution)/shard_map/ppermute | solution.py:478
  8.1 5.0 %collective-permute-start.3 = (f32[264,128]{1,0:T(8,128)S(1)}, f32[264,128]{1,0:T(8,128)S(1)}, u32[]{:S(2)}, u32[]{:S(2)}) collective-permute-start(f32[264,128]{1,0:T(8,128)S(1)} %get-tuple-element.37), channel_id=1, source_target_pairs={{1,2},{2,1},{3,4},{4,3},{5,6},{6,5},{7,8},{8,7},{9,10},{10,9},{11,... | collective-permute-start | bytes 405512 | tf_op jit(solution)/shard_map/ppermute | solution.py:477
  9.6 21.7 %copy-start = (s32[1,2,3]{2,1,0:T(2,128)S(1)}, s32[1,2,3]{2,1,0:T(2,128)}, u32[]{:S(2)}) copy-start(s32[1,2,3]{2,1,0:T(2,128)} %sends.1) | copy-start | bytes 76
  10.7 2.9 %collective-permute-start.4 = (f32[256,128]{1,0:T(8,128)S(1)}, f32[256,128]{1,0:T(8,128)S(1)}, u32[]{:S(2)}, u32[]{:S(2)}) collective-permute-start(f32[256,128]{1,0:T(8,128)S(1)} %get-tuple-element.41), channel_id=1, source_target_pairs={{0,1},{1,0},{2,3},{3,2},{4,5},{5,4},{6,7},{7,6},{8,9},{9,8},{10,11... | collective-permute-start | bytes 393224 | tf_op jit(solution)/shard_map/ppermute | solution.py:478
  10.9 5.0 %collective-permute-start.5 = (f32[256,128]{1,0:T(8,128)S(1)}, f32[256,128]{1,0:T(8,128)S(1)}, u32[]{:S(2)}, u32[]{:S(2)}) collective-permute-start(f32[256,128]{1,0:T(8,128)S(1)} %get-tuple-element.42), channel_id=1, source_target_pairs={{1,2},{2,1},{3,4},{4,3},{5,6},{6,5},{7,8},{8,7},{9,10},{10,9},{11,... | collective-permute-start | bytes 393224 | tf_op jit(solution)/shard_map/ppermute | solution.py:477
  17.6 13.6 %collective-permute-start.6 = (f32[256,128]{1,0:T(8,128)S(1)}, f32[256,128]{1,0:T(8,128)S(1)}, u32[]{:S(2)}, u32[]{:S(2)}) collective-permute-start(f32[256,128]{1,0:T(8,128)S(1)} %get-tuple-element.46), channel_id=1, source_target_pairs={{0,1},{1,0},{2,3},{3,2},{4,5},{5,4},{6,7},{7,6},{8,9},{9,8},{10,11... | collective-permute-start | bytes 393224 | tf_op jit(solution)/shard_map/ppermute | solution.py:478
  17.7 13.5 %collective-permute-start.7 = (f32[256,128]{1,0:T(8,128)S(1)}, f32[256,128]{1,0:T(8,128)S(1)}, u32[]{:S(2)}, u32[]{:S(2)}) collective-permute-start(f32[256,128]{1,0:T(8,128)S(1)} %get-tuple-element.47), channel_id=1, source_target_pairs={{1,2},{2,1},{3,4},{4,3},{5,6},{6,5},{7,8},{8,7},{9,10},{10,9},{11,... | collective-permute-start | bytes 393224 | tf_op jit(solution)/shard_map/ppermute | solution.py:477

commit v3 on v2

--- a/solution.py
+++ b/solution.py
@@ -220,7 +220,7 @@
 
 def build_kernel(
     sends_in, cols_in, cap_in, var_in, base, field_p,
-    w_high, w_low, flux_own, outer_out, near, far, coef_own, coef_halo, cap_p,
+    w_high, w_low, flux_own, outer_out, near, far, coef_own, cap_p,
     buf, acc, dense, major, result, weights_p, sends, cols, cap, var, place, sems,
 ):
     blocks, slots, flat = base.shape
@@ -256,9 +256,8 @@
         cap_p[:, lanes] = permute_blocks(cap, order, chunk, 1)
     weights = weights_p[...]
     value = field_p[...]
-    for coef in (coef_own, coef_halo):
-        coef[...] = jnp.zeros_like(coef)
-        set_coefs(coef, 0, jnp.ones((1, nodes), F32), weights)
+    coef_own[...] = jnp.zeros_like(coef_own)
+    set_coefs(coef_own, 0, jnp.ones((1, nodes), F32), weights)
     to_terms(major, value, value)
     couple(major, result, coef_list(coef_own))
 
@@ -298,8 +297,7 @@
 
     left = jnp.concatenate([marked(from_terms(result, 1)[0], terms), weights], axis=0)
     flux = product(*split(left), w_high[...], w_low[...], ((1,), (0,)))
-    for coef, first, lanes in ((coef_own, chunks, slice(0, nodes)), (coef_halo, chunks, slice(nodes, 2 * nodes))):
-        set_coefs(coef, first, flux[terms : terms + 1, lanes], flux[tall : tall + VARS, lanes])
+    set_coefs(coef_own, chunks, flux[terms : terms + 1, 0:nodes], flux[tall : tall + VARS, 0:nodes])
     flux_own[...] = flux[0:tall, 0:nodes]
     outer = flux[:, nodes:]
     outer_out[...] = outer
@@ -325,67 +323,61 @@
     store_sides(near, far, pack(own, False), pack(own, True))
 
 
-def flux_kernel(field, halo, outer, got_near, got_far, inward, outward, coef, major, result):
+def flux_kernel(
+    w_high, w_low, field, halo, outer, local, cap, coef_own, got_near, got_far,
+    image, outward, part, outer2, near, far, coef, coef2, major, result, major2, result2,
+):
     tall, nodes = field.shape
     terms = len(chaos_links())
+    chunks = nodes // LANES
     below, above = by_side(got_near[...], got_far[...])
     inflow = unpack(above, below)
     outer = outer[...]
     coef[...] = jnp.zeros_like(coef)
-    for first, flux in ((0, inflow), (nodes // LANES, outer)):
-        set_coefs(coef, first, flux[terms : terms + 1, :], flux[tall : tall + VARS, :])
+    coef2[...] = jnp.zeros_like(coef2)
+    transfer = (inflow[terms : terms + 1, :], inflow[tall : tall + VARS, :])
+    set_coefs(coef, 0, *transfer)
+    set_coefs(coef, chunks, outer[terms : terms + 1, :], outer[tall : tall + VARS, :])
+    set_coefs(coef2, chunks, *transfer)
+    coef2[...] = coef2[...] + coef_own[...]
     to_terms(major, field[...], halo[...])
     couple(major, result, coef_list(coef))
     own, other = from_terms(result, 2)
     row = row_iota(own.shape)
-    inward[...] = jnp.where(row < terms, own - inflow[0:tall], 0.0)
     outward[...] = jnp.where(row < terms, other - outer[0:tall], 0.0)
+    value = local[...] + jnp.where(row < terms, own - inflow[0:tall], 0.0)
+    image[...] = value
+    to_terms(major2, value, value)
+    couple(major2, result2, coef_list(coef2))
+    coupled, transferred = from_terms(result2, 2)
+    coupled = split(jnp.where(row < terms, coupled, 0.0))
+    flux = product(*coupled, w_high[...], w_low[...], ((1,), (0,)))
+    part[...] = jnp.where(row < terms, cap[...] * value + transferred - flux[:, 0:nodes], 0.0)
+    outer = flux[:, nodes:]
+    outer2[...] = outer
+    store_sides(near, far, pack(outer, True), pack(outer, False))
 
 
 def second_kernel(
     peers,
-    w_high, w_low, field, local, inward, outward, cap, coef_own, coef_halo, got_near, got_far,
-    image, local2, near, far, dots, major, result, major2, result2,
+    w_high, w_low, field, image, outward, part, outer2, coef_own, got_near, got_far,
+    local2, dots, major, result,
 ):
-    _, nodes = field.shape
     terms = len(chaos_links())
-    value = local[...] + inward[...]
+    value = image[...]
     halo = unpack(*by_side(got_near[...], got_far[...])) + outward[...]
     row = row_iota(value.shape)
-    image[...] = value
-    to_terms(major, value, value)
     extended = split(marked(jnp.concatenate([value, halo], axis=1), terms))
-    coefs = coef_list(coef_own)
-    mixed = []
-    cuts = list(range(0, nodes, 2 * LANES))
-    for part, start in enumerate(cuts):
-        span = slice(start, min(start + 2 * LANES, nodes))
-        mixed.append(product(*extended, w_high[span, :], w_low[span, :], ((1,), (1,))))
-        couple(major, result, coefs, part, len(cuts))
-    mixed = jnp.concatenate(mixed, axis=1)
-    to_terms(major2, mixed[terms : terms + 1, :] * value - mixed, halo)
-    coupled, transferred = from_terms(result, 2)
-    coupled = split(jnp.where(row < terms, coupled, 0.0))
-    coefs = coef_list(coef_halo)
-    flux = []
-    cuts = list(range(0, 2 * nodes, 2 * LANES))
-    for part, start in enumerate(cuts):
-        span = slice(start, start + 2 * LANES)
-        flux.append(product(*coupled, w_high[:, span], w_low[:, span], ((1,), (0,))))
-        couple(major2, result2, coefs, part, len(cuts))
-    flux = jnp.concatenate(flux, axis=1)
-    forward, outer = from_terms(result2, 2)
-    own = cap[...] * value + transferred + forward - flux[:, 0:nodes]
-    own = jnp.where(row < terms, own, 0.0)
-    outer = outer - flux[:, nodes:]
-    outer = jnp.where(row < terms, outer, 0.0)
+    mixed = product(*extended, w_high[...], w_low[...], ((1,), (1,)))
+    to_terms(major, mixed[terms : terms + 1, :] * value - mixed)
+    couple(major, result, coef_list(coef_own))
+    own = jnp.where(row < terms, part[...] + from_terms(result, 1)[0], 0.0)
     local2[...] = own
-    store_sides(near, far, pack(outer, True), pack(outer, False))
     sums = [
         lane_dot(field[...], field[...]),
         lane_dot(field[...], value),
         lane_dot(value, value),
-        lane_dot(value, own) + lane_dot(halo, outer),
+        lane_dot(value, own) - lane_dot(halo, outer2[...]),
     ]
     lane = lane_iota((1, LANES))
     packed = jnp.zeros((1, LANES), F32)
@@ -438,7 +430,7 @@
     put(0, solution_out)
     below, above = by_side(got_near[...], got_far[...])
     inward = unpack(above, below)
-    work[1] = field[...] - c1 * image[...] + c2 * (local2[...] + inward)
+    work[1] = field[...] - c1 * image[...] + c2 * (local2[...] - inward)
     put(1, residual_out)
     for copy in copies:
         copy.wait()
@@ -510,11 +502,11 @@
 
     tallest = shape((tall + VARS, nodes))
     deep = shape((packed_rows(tall + VARS), LANES))
-    w_high, w_low, flux_own, outer, near, far, coef_own, coef_halo, cap = pl.pallas_call(
+    w_high, w_low, flux_own, outer, near, far, coef_own, cap = pl.pallas_call(
         build_kernel,
-        out_shape=(weights, weights, wide, tallest, deep, deep, coefs, coefs, shape((1, nodes))),
+        out_shape=(weights, weights, wide, tallest, deep, deep, coefs, shape((1, nodes))),
         in_specs=hbm(5) + vmem(1),
-        out_specs=tuple(vmem(9)),
+        out_specs=tuple(vmem(8)),
         scratch_shapes=[
             pltpu.VMEM((blocks, slots, flat), F32),
             [pltpu.VMEM((2 * blocks, steps, LANES), F32) for _ in range(blocks)],
@@ -546,26 +538,26 @@
         name="local",
     )(w_high, w_low, field, flux_own, cap, coef_own, *got)
     got = exchange(near, far)
-    inward, outward = pl.pallas_call(
+    image, outward, part, outer2, near, far = pl.pallas_call(
         flux_kernel,
-        out_shape=(wide, wide),
-        in_specs=vmem(5),
-        out_specs=tuple(vmem(2)),
-        scratch_shapes=[pltpu.VMEM(coefs.shape, F32)] + [spread] * 2,
+        out_shape=(wide, wide, wide, wide, piece, piece),
+        in_specs=vmem(10),
+        out_specs=tuple(vmem(6)),
+        scratch_shapes=[pltpu.VMEM(coefs.shape, F32)] * 2 + [spread] * 4,
         compiler_params=params,
         name="flux",
-    )(field, halo, outer, *got_flux)
-
-    image, local2, near, far, dots = pl.pallas_call(
+    )(w_high, w_low, field, halo, outer, local, cap, coef_own, *got_flux)
+    got_flux = exchange(near, far)
+
+    local2, dots = pl.pallas_call(
         functools.partial(second_kernel, peers),
-        out_shape=(wide, wide, piece, piece, shape((peers, 1, LANES))),
-        in_specs=vmem(11),
-        out_specs=tuple(vmem(5)),
-        scratch_shapes=[spread] * 4,
+        out_shape=(wide, shape((peers, 1, LANES))),
+        in_specs=vmem(10),
+        out_specs=tuple(vmem(2)),
+        scratch_shapes=[spread] * 2,
         compiler_params=params,
         name="second",
-    )(w_high, w_low, field, local, inward, outward, cap, coef_own, coef_halo, *got)
-    got = exchange(near, far)
+    )(w_high, w_low, field, image, outward, part, outer2, coef_own, *got)
     gathered = lax.all_to_all(dots, "space", 0, 0, tiled=True)
 
     return pl.pallas_call(
@@ -581,7 +573,7 @@
         ],
         compiler_params=params,
         name="finish",
-    )(send_list, gathered, field, image, local2, *got)
+    )(send_list, gathered, field, image, local2, *got_flux)
 
 
 def solution(mesh):

time: 33.6 us -> 32.7 us (0.973)
  blocking collectives: 12.1 us -> 0 us
  starting transfers between devices: 8.07 us -> 13.9 us
  waiting for transfers between devices: 3.02 us -> 7.07 us
  Pallas kernels: 9.54 us -> 10.7 us
    all_to_all x1 -> x0, blocking collectives: 12.1 us -> none  [shards(): gathered = lax.all_to_all(dots, 'space', 0, 0, tiled=True)]
    all_to_all x0 -> x1, waiting for transfers between devices: none -> 6.34 us  [shards(): gathered = lax.all_to_all(dots, 'space', 0, 0, tiled=True)]
    all_to_all x0 -> x1, starting transfers between devices: none -> 5.79 us  [shards(): gathered = lax.all_to_all(dots, 'space', 0, 0, tiled=True)]
    ppermute x4, waiting for transfers between devices: 3.01 us -> 0.72 us  [exchange(): got_far = lax.ppermute(far, ('grp', 'space'), outer)]
    pallas_call x1, Pallas kernels: 0.48 us -> 1.67 us  [shards(): pl.pallas_call(flux_kernel, out_shape=(wide, wide, wide, wide, piece, pie...]
  transfers between devices with their start and end apart: 8 -> 9, of which waited for: 2 -> 2; matrix products, arithmetic and copies ran while one was open for 0% -> 0% of each run, Pallas kernels for 14% -> 23%
where the time goes in v3:
time: 32.7 us; the launch traced here: 32.4 us
  starting transfers between devices  13.9 us (43%)
  Pallas kernels  10.7 us (33%)
  waiting for transfers between devices  7.07 us (22%)
  between operations  0.69 us (2%)
    ppermute x4, starting transfers between devices, exchange(): got_far = lax.ppermute(far, ('grp', 'space'), outer)  7.02 us
    all_to_all x1, waiting for transfers between devices, shards(): gathered = lax.all_to_all(dots, 'space', 0, 0, tiled=True)  6.34 us
    all_to_all x1, starting transfers between devices, shards(): gathered = lax.all_to_all(dots, 'space', 0, 0, tiled=True)  5.79 us
    pallas_call x1, Pallas kernels, shards(): pl.pallas_call(build_kernel, out_shape=(weights, weights, wide, tallest,...  2.94 us
    pallas_call x1, Pallas kernels, shards(): pl.pallas_call(functools.partial(final_kernel, peers), out_shape=(shape((...  2.08 us
    pallas_call x1, Pallas kernels, shards(): pl.pallas_call(functools.partial(second_kernel, peers), out_shape=(wide,...  1.79 us
    pallas_call x1, Pallas kernels, shards(): pl.pallas_call(flux_kernel, out_shape=(wide, wide, wide, wide, piece, pie...  1.67 us
    pallas_call x1, Pallas kernels, shards(): pl.pallas_call(send_kernel, out_shape=(wide, piece, piece), in_specs=hbm(...  1.2 us
  transfers between devices with their start and end apart: 9, of which 2 were waited for; matrix products, arithmetic and copies ran while one was open for 0% of the time, Pallas kernels for 23%

profile of v3, /device:TPU:0, one launch (start us, length us, event | category | flops | bytes accessed | tf_op | source)
XLA Modules:
  0.0 32.4 jit_solution(8854998554454782936)
XLA Ops:
  0.6 1.2 %send.1 = (f32[168,384]{1,0:T(8,128)S(1)}, f32[256,128]{1,0:T(8,128)S(1)}, f32[256,128]{1,0:T(8,128)S(1)}) custom-call(s32[1,2,3]{2,1,0:T(2,128)} %sends.1, f32[165,384]{1,0:T(8,128)} %field_in.1), custom_call_target="tpu_custom_call" | custom-call | tf_op jit(solution)/shard_map/send/pallas_call | solution.py:488
  1.8 0.6 %collective-permute-start = (f32[256,128]{1,0:T(8,128)S(1)}, f32[256,128]{1,0:T(8,128)S(1)}, u32[]{:S(2)}, u32[]{:S(2)}) collective-permute-start(f32[256,128]{1,0:T(8,128)S(1)} %get-tuple-element.31), channel_id=1, source_target_pairs={{0,1},{1,0},{2,3},{3,2},{4,5},{5,4},{6,7},{7,6},{8,9},{9,8},{10,11... | collective-permute-start | bytes 393224 | tf_op jit(solution)/shard_map/ppermute | solution.py:470
  2.4 2.6 %collective-permute-start.1 = (f32[256,128]{1,0:T(8,128)S(1)}, f32[256,128]{1,0:T(8,128)S(1)}, u32[]{:S(2)}, u32[]{:S(2)}) collective-permute-start(f32[256,128]{1,0:T(8,128)S(1)} %get-tuple-element.32), channel_id=1, source_target_pairs={{1,2},{2,1},{3,4},{4,3},{5,6},{6,5},{7,8},{8,7},{9,10},{10,9},{11,... | collective-permute-start | bytes 393224 | tf_op jit(solution)/shard_map/ppermute | solution.py:469
  4.9 2.9 %build.1 = (bf16[384,768]{1,0:T(8,128)(2,1)S(1)}, bf16[384,768]{1,0:T(8,128)(2,1)S(1)}, f32[168,384]{1,0:T(8,128)S(1)}, f32[176,384]{1,0:T(8,128)S(1)}, f32[264,...) custom-call(s32[1,2,3]{2,1,0:T(2,128)} %sends.1, s32[6,23]{1,0:T(8,128)} %cols_in.1, ...), custom_call_target="tpu_custom_call" | custom-call | flops 1000000000 | bytes 4000000 | tf_op jit(solution)/shard_map/build/pallas_call | solution.py:505
  7.9 0.2 collective-permute-start.2
  8.1 1.5 %collective-permute-start.3 = (f32[264,128]{1,0:T(8,128)S(1)}, f32[264,128]{1,0:T(8,128)S(1)}, u32[]{:S(2)}, u32[]{:S(2)}) collective-permute-start(f32[264,128]{1,0:T(8,128)S(1)} %get-tuple-element.37), channel_id=1, source_target_pairs={{1,2},{2,1},{3,4},{4,3},{5,6},{6,5},{7,8},{8,7},{9,10},{10,9},{11,... | collective-permute-start | bytes 405512 | tf_op jit(solution)/shard_map/ppermute | solution.py:469
  9.6 0.0 collective-permute-done.got_near
  9.6 0.0 collective-permute-done.1.got_far
  9.6 1.1 %local.1 = (f32[168,384]{1,0:T(8,128)S(1)}, f32[168,384]{1,0:T(8,128)S(1)}, f32[256,128]{1,0:T(8,128)S(1)}, f32[256,128]{1,0:T(8,128)S(1)}) custom-call(bf16[384,768]{1,0:T(8,128)(2,1)S(1)} %get-tuple-element.26.w_high, bf16[384,768]{1,0:T(8,128)(2,1)S(1)} %get-tuple-element.27.w_low, f32[168,384]{1,0:T(8,128)S(1)} %get-tuple-element.25.field_p.field, ...), custom_call_target="tpu_custom_call" | custom-call | tf_op jit(solution)/shard_map/local/pallas_call | solution.py:531
  10.7 0.2 collective-permute-start.4
  10.9 1.5 %collective-permute-start.5 = (f32[256,128]{1,0:T(8,128)S(1)}, f32[256,128]{1,0:T(8,128)S(1)}, u32[]{:S(2)}, u32[]{:S(2)}) collective-permute-start(f32[256,128]{1,0:T(8,128)S(1)} %get-tuple-element.43), channel_id=1, source_target_pairs={{1,2},{2,1},{3,4},{4,3},{5,6},{6,5},{7,8},{8,7},{9,10},{10,9},{11,... | collective-permute-start | bytes 393224 | tf_op jit(solution)/shard_map/ppermute | solution.py:469
  12.4 0.0 collective-permute-done.2.got_near
  12.4 0.7 %collective-permute-done.3.got_far = f32[264,128]{1,0:T(8,128)S(1)} collective-permute-done((f32[264,128]{1,0:T(8,128)S(1)}, f32[264,128]{1,0:T(8,128)S(1)}, u32[]{:S(2)}, u32[]{:S(2)}) %collective-permute-start.3) | collective-permute-done | bytes 135200 | tf_op jit(solution)/shard_map/ppermute | solution.py:469
  13.1 1.7 %flux.1 = (f32[168,384]{1,0:T(8,128)S(1)}, f32[168,384]{1,0:T(8,128)S(1)}, f32[168,384]{1,0:T(8,128)S(1)}, f32[168,384]{1,0:T(8,128)S(1)}, f32[256,128]{1,0:T(8,128)S(1)}, /*index=5*/f32[256,128]{1,0:T(8,128)S(1)}) custom-call(bf16[384,768]{1,0:T(8,128)(2,1)S(1)} %get-tuple-element.26.w_high, bf16[384,768]{1,0:T(8,128)(2,1)S(1)} %get-tuple-element.27.w_low, ...), custom_call_target="tpu_custom_call" | custom-call | tf_op jit(solution)/shard_map/flux/pallas_call | solution.py:541
  14.7 0.2 collective-permute-start.6
  14.9 1.5 %collective-permute-start.7 = (f32[256,128]{1,0:T(8,128)S(1)}, f32[256,128]{1,0:T(8,128)S(1)}, u32[]{:S(2)}, u32[]{:S(2)}) collective-permute-start(f32[256,128]{1,0:T(8,128)S(1)} %get-tuple-element.47), channel_id=1, source_target_pairs={{1,2},{2,1},{3,4},{4,3},{5,6},{6,5},{7,8},{8,7},{9,10},{10,9},{11,... | collective-permute-start | bytes 393224 | tf_op jit(solution)/shard_map/ppermute | solution.py:469
  16.4 0.0 collective-permute-done.4.got_near
  16.4 0.0 collective-permute-done.5.got_far
  16.4 1.8 %second.1 = (f32[168,384]{1,0:T(8,128)S(1)}, f32[16,1,128]{2,1,0:T(1,128)}) custom-call(bf16[384,768]{1,0:T(8,128)(2,1)S(1)} %get-tuple-element.26.w_high, bf16[384,768]{1,0:T(8,128)(2,1)S(1)} %get-tuple-element.27.w_low, f32[168,384]{1,0:T(8,128)S(1)} %get-tuple-element.25.field_p.field, f32[168,384]{1,0:T(8,128)S(1)} %get-tuple-element.38.image, ...), custom_call_target="tpu_custom_call" | custom-call | tf_op jit(solution)/shard_map/second/pallas_call | solution.py:552
  18.2 5.8 %all-to-all-start = ((f32[16,1,128]{2,1,0:T(1,128)}), f32[16,1,128]{2,1,0:T(1,128)S(1)}, u32[]{:S(2)}, u32[]{:S(2)}) async-start(f32[16,1,128]{2,1,0:T(1,128)} %get-tuple-element.44), calls=%async_computation | async-start | bytes 16384 | tf_op jit(solution)/shard_map/all_to_all | solution.py:561
  24.0 0.0 collective-permute-done.6.got_near
  24.0 0.0 collective-permute-done.7.got_far
  24.0 6.3 %all-to-all-done.dots = f32[16,1,128]{2,1,0:T(1,128)S(1)} async-done(((f32[16,1,128]{2,1,0:T(1,128)}), f32[16,1,128]{2,1,0:T(1,128)S(1)}, u32[]{:S(2)}, u32[]{:S(2)}) %all-to-all-start) | async-done | bytes 8224 | tf_op jit(solution)/shard_map/all_to_all | solution.py:561
  30.4 2.1 %finish.1 = (f32[165,384]{1,0:T(8,128)}, f32[165,384]{1,0:T(8,128)}) custom-call(s32[1,2,3]{2,1,0:T(2,128)S(1)} %copy-done, f32[16,1,128]{2,1,0:T(1,128)S(1)} %all-to-all-done.dots, f32[168,384]{1,0:T(8,128)S(1)} %get-tuple-element.25.field_p.field, f32[168,384]{1,0:T(8,128)S(1)} %get-tuple-element.38.image, f32[168,384]{1,0:T(8,128)S(1)} %get-tuple-element.45.local2, ...), custom_call_target="tpu_custom_call" | custom-call | tf_op jit(solution)/shard_map/finish/pallas_call | solution.py:563
  (2 shorter events, 0.0 us)
Async XLA Ops:
  1.8 7.7 %collective-permute-start = (f32[256,128]{1,0:T(8,128)S(1)}, f32[256,128]{1,0:T(8,128)S(1)}, u32[]{:S(2)}, u32[]{:S(2)}) collective-permute-start(f32[256,128]{1,0:T(8,128)S(1)} %get-tuple-element.31), channel_id=1, source_target_pairs={{0,1},{1,0},{2,3},{3,2},{4,5},{5,4},{6,7},{7,6},{8,9},{9,8},{10,11... | collective-permute-start | bytes 393224 | tf_op jit(solution)/shard_map/ppermute | solution.py:470
  2.4 7.2 %collective-permute-start.1 = (f32[256,128]{1,0:T(8,128)S(1)}, f32[256,128]{1,0:T(8,128)S(1)}, u32[]{:S(2)}, u32[]{:S(2)}) collective-permute-start(f32[256,128]{1,0:T(8,128)S(1)} %get-tuple-element.32), channel_id=1, source_target_pairs={{1,2},{2,1},{3,4},{4,3},{5,6},{6,5},{7,8},{8,7},{9,10},{10,9},{11,... | collective-permute-start | bytes 393224 | tf_op jit(solution)/shard_map/ppermute | solution.py:469
  7.9 4.5 %collective-permute-start.2 = (f32[264,128]{1,0:T(8,128)S(1)}, f32[264,128]{1,0:T(8,128)S(1)}, u32[]{:S(2)}, u32[]{:S(2)}) collective-permute-start(f32[264,128]{1,0:T(8,128)S(1)} %get-tuple-element.36), channel_id=1, source_target_pairs={{0,1},{1,0},{2,3},{3,2},{4,5},{5,4},{6,7},{7,6},{8,9},{9,8},{10,11... | collective-permute-start | bytes 405512 | tf_op jit(solution)/shard_map/ppermute | solution.py:470
  8.1 5.0 %collective-permute-start.3 = (f32[264,128]{1,0:T(8,128)S(1)}, f32[264,128]{1,0:T(8,128)S(1)}, u32[]{:S(2)}, u32[]{:S(2)}) collective-permute-start(f32[264,128]{1,0:T(8,128)S(1)} %get-tuple-element.37), channel_id=1, source_target_pairs={{1,2},{2,1},{3,4},{4,3},{5,6},{6,5},{7,8},{8,7},{9,10},{10,9},{11,... | collective-permute-start | bytes 405512 | tf_op jit(solution)/shard_map/ppermute | solution.py:469
  10.7 5.8 %collective-permute-start.4 = (f32[256,128]{1,0:T(8,128)S(1)}, f32[256,128]{1,0:T(8,128)S(1)}, u32[]{:S(2)}, u32[]{:S(2)}) collective-permute-start(f32[256,128]{1,0:T(8,128)S(1)} %get-tuple-element.42), channel_id=1, source_target_pairs={{0,1},{1,0},{2,3},{3,2},{4,5},{5,4},{6,7},{7,6},{8,9},{9,8},{10,11... | collective-permute-start | bytes 393224 | tf_op jit(solution)/shard_map/ppermute | solution.py:470
  10.9 5.5 %collective-permute-start.5 = (f32[256,128]{1,0:T(8,128)S(1)}, f32[256,128]{1,0:T(8,128)S(1)}, u32[]{:S(2)}, u32[]{:S(2)}) collective-permute-start(f32[256,128]{1,0:T(8,128)S(1)} %get-tuple-element.43), channel_id=1, source_target_pairs={{1,2},{2,1},{3,4},{4,3},{5,6},{6,5},{7,8},{8,7},{9,10},{10,9},{11,... | collective-permute-start | bytes 393224 | tf_op jit(solution)/shard_map/ppermute | solution.py:469
  13.1 17.3 %copy-start = (s32[1,2,3]{2,1,0:T(2,128)S(1)}, s32[1,2,3]{2,1,0:T(2,128)}, u32[]{:S(2)}) copy-start(s32[1,2,3]{2,1,0:T(2,128)} %sends.1) | copy-start | bytes 76
  14.7 9.3 %collective-permute-start.6 = (f32[256,128]{1,0:T(8,128)S(1)}, f32[256,128]{1,0:T(8,128)S(1)}, u32[]{:S(2)}, u32[]{:S(2)}) collective-permute-start(f32[256,128]{1,0:T(8,128)S(1)} %get-tuple-element.46), channel_id=1, source_target_pairs={{0,1},{1,0},{2,3},{3,2},{4,5},{5,4},{6,7},{7,6},{8,9},{9,8},{10,11... | collective-permute-start | bytes 393224 | tf_op jit(solution)/shard_map/ppermute | solution.py:470
  14.9 9.1 %collective-permute-start.7 = (f32[256,128]{1,0:T(8,128)S(1)}, f32[256,128]{1,0:T(8,128)S(1)}, u32[]{:S(2)}, u32[]{:S(2)}) collective-permute-start(f32[256,128]{1,0:T(8,128)S(1)} %get-tuple-element.47), channel_id=1, source_target_pairs={{1,2},{2,1},{3,4},{4,3},{5,6},{6,5},{7,8},{8,7},{9,10},{10,9},{11,... | collective-permute-start | bytes 393224 | tf_op jit(solution)/shard_map/ppermute | solution.py:469
  18.2 12.2 %all-to-all-start = ((f32[16,1,128]{2,1,0:T(1,128)}), f32[16,1,128]{2,1,0:T(1,128)S(1)}, u32[]{:S(2)}, u32[]{:S(2)}) async-start(f32[16,1,128]{2,1,0:T(1,128)} %get-tuple-element.44), calls=%async_computation | async-start | bytes 16384 | tf_op jit(solution)/shard_map/all_to_all | solution.py:561

commit v4 on v3

--- a/solution.py
+++ b/solution.py
@@ -389,16 +389,7 @@
         dots[peer] = packed
 
 
-def final_kernel(
-    peers, sends, dots, field, image, local2, got_near, got_far,
-    solution_out, residual_out, place, work, out, sems,
-):
-    terms, nodes = solution_out.shape
-    order = order_of(sends)
-    blocks = len(order)
-    for j in range(blocks):
-        place[order[j]] = j
-    places = [place[j] for j in range(blocks)]
+def step_kernel(peers, dots, steps):
     total = dots[0]
     for peer in range(1, peers):
         total = total + dots[peer]
@@ -417,6 +408,20 @@
     step1 = norm1 / curve
     c1 = step0 + step1 * grow
     c2 = step0 * step1
+    steps[...] = jnp.where(row_iota(steps.shape) == 0, c1, c2)
+
+
+def final_kernel(
+    sends, steps, field, image, local2, got_near, got_far,
+    solution_out, residual_out, place, work, out, sems,
+):
+    terms, nodes = solution_out.shape
+    order = order_of(sends)
+    blocks = len(order)
+    for j in range(blocks):
+        place[order[j]] = j
+    places = [place[j] for j in range(blocks)]
+    c1, c2 = steps[0:1, 0:1], steps[1:2, 0:1]
     copies = []
 
     def put(which, target):
@@ -560,8 +565,17 @@
     )(w_high, w_low, field, image, outward, part, outer2, coef_own, *got)
     gathered = lax.all_to_all(dots, "space", 0, 0, tiled=True)
 
+    step_sizes = pl.pallas_call(
+        functools.partial(step_kernel, peers),
+        out_shape=shape((8, LANES)),
+        in_specs=vmem(1),
+        out_specs=vmem(1)[0],
+        compiler_params=params,
+        name="step",
+    )(gathered)
+
     return pl.pallas_call(
-        functools.partial(final_kernel, peers),
+        final_kernel,
         out_shape=(shape((terms, nodes)), shape((terms, nodes))),
         in_specs=smem(1) + vmem(6),
         out_specs=tuple(hbm(2)),
@@ -573,7 +587,7 @@
         ],
         compiler_params=params,
         name="finish",
-    )(send_list, gathered, field, image, local2, *got_flux)
+    )(send_list, step_sizes, field, image, local2, *got_flux)
 
 
 def solution(mesh):

time: 32.7 us -> 32 us (0.979)
  blocking collectives: 0 us -> 12 us
  waiting for transfers between devices: 7.07 us -> 0.72 us
  starting transfers between devices: 13.9 us -> 8.16 us
  Pallas kernels: 10.7 us -> 10.2 us
    all_to_all x0 -> x1, blocking collectives: none -> 12 us  [shards(): gathered = lax.all_to_all(dots, 'space', 0, 0, tiled=True)]
    all_to_all x1 -> x0, waiting for transfers between devices: 6.34 us -> none  [shards(): gathered = lax.all_to_all(dots, 'space', 0, 0, tiled=True)]
    all_to_all x1 -> x0, starting transfers between devices: 5.79 us -> none  [shards(): gathered = lax.all_to_all(dots, 'space', 0, 0, tiled=True)]
    pallas_call x1, Pallas kernels: 1.79 us -> 1.2 us  [shards(): pl.pallas_call(functools.partial(second_kernel, peers), out_shape=(wide,...]
    pallas_call x1 -> x2, Pallas kernels: 2.08 us -> 2.15 us  [the longest x1 1.83 us: shards(): pl.pallas_call(final_kernel, out_shape=(shape((terms, nodes)), shape((ter...]
  transfers between devices with their start and end apart: 9 -> 8, of which waited for: 2 -> 1; matrix products, arithmetic and copies ran while one was open for 0% -> 0% of each run, Pallas kernels for 23% -> 23%
where the time goes in v4:
time: 32 us; the launch traced here: 31.8 us
  blocking collectives  12 us (38%)
  Pallas kernels  10.2 us (32%)
  starting transfers between devices  8.16 us (26%)
  waiting for transfers between devices  0.72 us (2%)
  between operations  0.68 us (2%)
    all_to_all x1, blocking collectives, shards(): gathered = lax.all_to_all(dots, 'space', 0, 0, tiled=True)  12 us
    ppermute x4, starting transfers between devices, exchange(): got_far = lax.ppermute(far, ('grp', 'space'), outer)  7.01 us
    pallas_call x1, Pallas kernels, shards(): pl.pallas_call(build_kernel, out_shape=(weights, weights, wide, tallest,...  2.94 us
    pallas_call x1, Pallas kernels, shards(): pl.pallas_call(final_kernel, out_shape=(shape((terms, nodes)), shape((ter...  1.83 us
    pallas_call x1, Pallas kernels, shards(): pl.pallas_call(flux_kernel, out_shape=(wide, wide, wide, wide, piece, pie...  1.65 us
    pallas_call x1, Pallas kernels, shards(): pl.pallas_call(send_kernel, out_shape=(wide, piece, piece), in_specs=hbm(...  1.2 us
    pallas_call x1, Pallas kernels, shards(): pl.pallas_call(functools.partial(second_kernel, peers), out_shape=(wide,...  1.2 us
    ppermute x4, starting transfers between devices, exchange(): got_near = lax.ppermute(near, 'space', inner)  1.15 us
  transfers between devices with their start and end apart: 8, of which 1 were waited for; matrix products, arithmetic and copies ran while one was open for 0% of the time, Pallas kernels for 23%

profile of v4, /device:TPU:0, one launch (start us, length us, event | category | flops | bytes accessed | tf_op | source)
XLA Modules:
  0.0 31.8 jit_solution(5973111815528029193)
XLA Ops:
  0.6 1.2 %send.1 = (f32[168,384]{1,0:T(8,128)S(1)}, f32[256,128]{1,0:T(8,128)S(1)}, f32[256,128]{1,0:T(8,128)S(1)}) custom-call(s32[1,2,3]{2,1,0:T(2,128)} %sends.1, f32[165,384]{1,0:T(8,128)} %field_in.1), custom_call_target="tpu_custom_call" | custom-call | tf_op jit(solution)/shard_map/send/pallas_call | solution.py:493
  1.8 0.6 %collective-permute-start = (f32[256,128]{1,0:T(8,128)S(1)}, f32[256,128]{1,0:T(8,128)S(1)}, u32[]{:S(2)}, u32[]{:S(2)}) collective-permute-start(f32[256,128]{1,0:T(8,128)S(1)} %get-tuple-element.31), channel_id=1, source_target_pairs={{0,1},{1,0},{2,3},{3,2},{4,5},{5,4},{6,7},{7,6},{8,9},{9,8},{10,11... | collective-permute-start | bytes 393224 | tf_op jit(solution)/shard_map/ppermute | solution.py:475
  2.4 2.6 %collective-permute-start.1 = (f32[256,128]{1,0:T(8,128)S(1)}, f32[256,128]{1,0:T(8,128)S(1)}, u32[]{:S(2)}, u32[]{:S(2)}) collective-permute-start(f32[256,128]{1,0:T(8,128)S(1)} %get-tuple-element.32), channel_id=1, source_target_pairs={{1,2},{2,1},{3,4},{4,3},{5,6},{6,5},{7,8},{8,7},{9,10},{10,9},{11,... | collective-permute-start | bytes 393224 | tf_op jit(solution)/shard_map/ppermute | solution.py:474
  4.9 2.9 %build.1 = (bf16[384,768]{1,0:T(8,128)(2,1)S(1)}, bf16[384,768]{1,0:T(8,128)(2,1)S(1)}, f32[168,384]{1,0:T(8,128)S(1)}, f32[176,384]{1,0:T(8,128)S(1)}, f32[264,...) custom-call(s32[1,2,3]{2,1,0:T(2,128)} %sends.1, s32[6,23]{1,0:T(8,128)} %cols_in.1, ...), custom_call_target="tpu_custom_call" | custom-call | flops 1000000000 | bytes 4000000 | tf_op jit(solution)/shard_map/build/pallas_call | solution.py:510
  7.9 0.2 collective-permute-start.2
  8.1 1.5 %collective-permute-start.3 = (f32[264,128]{1,0:T(8,128)S(1)}, f32[264,128]{1,0:T(8,128)S(1)}, u32[]{:S(2)}, u32[]{:S(2)}) collective-permute-start(f32[264,128]{1,0:T(8,128)S(1)} %get-tuple-element.37), channel_id=1, source_target_pairs={{1,2},{2,1},{3,4},{4,3},{5,6},{6,5},{7,8},{8,7},{9,10},{10,9},{11,... | collective-permute-start | bytes 405512 | tf_op jit(solution)/shard_map/ppermute | solution.py:474
  9.6 0.0 collective-permute-done.got_near
  9.6 0.0 collective-permute-done.1.got_far
  9.6 1.1 %local.1 = (f32[168,384]{1,0:T(8,128)S(1)}, f32[168,384]{1,0:T(8,128)S(1)}, f32[256,128]{1,0:T(8,128)S(1)}, f32[256,128]{1,0:T(8,128)S(1)}) custom-call(bf16[384,768]{1,0:T(8,128)(2,1)S(1)} %get-tuple-element.26.w_high, bf16[384,768]{1,0:T(8,128)(2,1)S(1)} %get-tuple-element.27.w_low, f32[168,384]{1,0:T(8,128)S(1)} %get-tuple-element.25.field_p.field, ...), custom_call_target="tpu_custom_call" | custom-call | tf_op jit(solution)/shard_map/local/pallas_call | solution.py:536
  10.7 0.2 collective-permute-start.4
  10.9 1.5 %collective-permute-start.5 = (f32[256,128]{1,0:T(8,128)S(1)}, f32[256,128]{1,0:T(8,128)S(1)}, u32[]{:S(2)}, u32[]{:S(2)}) collective-permute-start(f32[256,128]{1,0:T(8,128)S(1)} %get-tuple-element.43), channel_id=1, source_target_pairs={{1,2},{2,1},{3,4},{4,3},{5,6},{6,5},{7,8},{8,7},{9,10},{10,9},{11,... | collective-permute-start | bytes 393224 | tf_op jit(solution)/shard_map/ppermute | solution.py:474
  12.4 0.0 collective-permute-done.2.got_near
  12.4 0.7 %collective-permute-done.3.got_far = f32[264,128]{1,0:T(8,128)S(1)} collective-permute-done((f32[264,128]{1,0:T(8,128)S(1)}, f32[264,128]{1,0:T(8,128)S(1)}, u32[]{:S(2)}, u32[]{:S(2)}) %collective-permute-start.3) | collective-permute-done | bytes 135200 | tf_op jit(solution)/shard_map/ppermute | solution.py:474
  13.1 1.6 %flux.1 = (f32[168,384]{1,0:T(8,128)S(1)}, f32[168,384]{1,0:T(8,128)S(1)}, f32[168,384]{1,0:T(8,128)S(1)}, f32[168,384]{1,0:T(8,128)S(1)}, f32[256,128]{1,0:T(8,128)S(1)}, /*index=5*/f32[256,128]{1,0:T(8,128)S(1)}) custom-call(bf16[384,768]{1,0:T(8,128)(2,1)S(1)} %get-tuple-element.26.w_high, bf16[384,768]{1,0:T(8,128)(2,1)S(1)} %get-tuple-element.27.w_low, ...), custom_call_target="tpu_custom_call" | custom-call | tf_op jit(solution)/shard_map/flux/pallas_call | solution.py:546
  14.7 0.2 collective-permute-start.6
  14.9 1.5 %collective-permute-start.7 = (f32[256,128]{1,0:T(8,128)S(1)}, f32[256,128]{1,0:T(8,128)S(1)}, u32[]{:S(2)}, u32[]{:S(2)}) collective-permute-start(f32[256,128]{1,0:T(8,128)S(1)} %get-tuple-element.47), channel_id=1, source_target_pairs={{1,2},{2,1},{3,4},{4,3},{5,6},{6,5},{7,8},{8,7},{9,10},{10,9},{11,... | collective-permute-start | bytes 393224 | tf_op jit(solution)/shard_map/ppermute | solution.py:474
  16.4 0.0 collective-permute-done.4.got_near
  16.4 0.0 collective-permute-done.5.got_far
  16.4 1.2 %second.1 = (f32[168,384]{1,0:T(8,128)S(1)}, f32[16,1,128]{2,1,0:T(1,128)S(1)}) custom-call(bf16[384,768]{1,0:T(8,128)(2,1)S(1)} %get-tuple-element.26.w_high, bf16[384,768]{1,0:T(8,128)(2,1)S(1)} %get-tuple-element.27.w_low, f32[168,384]{1,0:T(8,128)S(1)} %get-tuple-element.25.field_p.field, f32[168,384]{1,0:T(8,128)S(1)} %get-tuple-element.38.image, ...), custom_call_target="tpu_custom_call" | custom-call | tf_op jit(solution)/shard_map/second/pallas_call | solution.py:557
  17.6 12.0 %all_to_all.5.dots = f32[16,1,128]{2,1,0:T(1,128)S(1)} all-to-all(f32[16,1,128]{2,1,0:T(1,128)S(1)} %get-tuple-element.44), channel_id=1, replica_groups=mesh['grp'=2,'space'=16] {'space'}, dimensions={0} | all-to-all | bytes 16384 | tf_op jit(solution)/shard_map/all_to_all | solution.py:566
  29.6 0.3 step.1.steps
  29.9 0.0 collective-permute-done.6.got_near
  29.9 0.0 collective-permute-done.7.got_far
  30.0 1.8 %finish.1 = (f32[165,384]{1,0:T(8,128)}, f32[165,384]{1,0:T(8,128)}) custom-call(s32[1,2,3]{2,1,0:T(2,128)S(1)} %copy-done, f32[8,128]{1,0:T(8,128)S(1)} %step.1.steps, f32[168,384]{1,0:T(8,128)S(1)} %get-tuple-element.25.field_p.field, f32[168,384]{1,0:T(8,128)S(1)} %get-tuple-element.38.image, f32[168,384]{1,0:T(8,128)S(1)} %get-tuple-element.45.local2, ...), custom_call_target="tpu_custom_call" | custom-call | tf_op jit(solution)/shard_map/finish/pallas_call | solution.py:577
  (2 shorter events, 0.0 us)
Async XLA Ops:
  1.8 7.7 %collective-permute-start = (f32[256,128]{1,0:T(8,128)S(1)}, f32[256,128]{1,0:T(8,128)S(1)}, u32[]{:S(2)}, u32[]{:S(2)}) collective-permute-start(f32[256,128]{1,0:T(8,128)S(1)} %get-tuple-element.31), channel_id=1, source_target_pairs={{0,1},{1,0},{2,3},{3,2},{4,5},{5,4},{6,7},{7,6},{8,9},{9,8},{10,11... | collective-permute-start | bytes 393224 | tf_op jit(solution)/shard_map/ppermute | solution.py:475
  2.4 7.2 %collective-permute-start.1 = (f32[256,128]{1,0:T(8,128)S(1)}, f32[256,128]{1,0:T(8,128)S(1)}, u32[]{:S(2)}, u32[]{:S(2)}) collective-permute-start(f32[256,128]{1,0:T(8,128)S(1)} %get-tuple-element.32), channel_id=1, source_target_pairs={{1,2},{2,1},{3,4},{4,3},{5,6},{6,5},{7,8},{8,7},{9,10},{10,9},{11,... | collective-permute-start | bytes 393224 | tf_op jit(solution)/shard_map/ppermute | solution.py:474
  7.9 4.5 %collective-permute-start.2 = (f32[264,128]{1,0:T(8,128)S(1)}, f32[264,128]{1,0:T(8,128)S(1)}, u32[]{:S(2)}, u32[]{:S(2)}) collective-permute-start(f32[264,128]{1,0:T(8,128)S(1)} %get-tuple-element.36), channel_id=1, source_target_pairs={{0,1},{1,0},{2,3},{3,2},{4,5},{5,4},{6,7},{7,6},{8,9},{9,8},{10,11... | collective-permute-start | bytes 405512 | tf_op jit(solution)/shard_map/ppermute | solution.py:475
  8.1 5.0 %collective-permute-start.3 = (f32[264,128]{1,0:T(8,128)S(1)}, f32[264,128]{1,0:T(8,128)S(1)}, u32[]{:S(2)}, u32[]{:S(2)}) collective-permute-start(f32[264,128]{1,0:T(8,128)S(1)} %get-tuple-element.37), channel_id=1, source_target_pairs={{1,2},{2,1},{3,4},{4,3},{5,6},{6,5},{7,8},{8,7},{9,10},{10,9},{11,... | collective-permute-start | bytes 405512 | tf_op jit(solution)/shard_map/ppermute | solution.py:474
  10.7 5.7 %collective-permute-start.4 = (f32[256,128]{1,0:T(8,128)S(1)}, f32[256,128]{1,0:T(8,128)S(1)}, u32[]{:S(2)}, u32[]{:S(2)}) collective-permute-start(f32[256,128]{1,0:T(8,128)S(1)} %get-tuple-element.42), channel_id=1, source_target_pairs={{0,1},{1,0},{2,3},{3,2},{4,5},{5,4},{6,7},{7,6},{8,9},{9,8},{10,11... | collective-permute-start | bytes 393224 | tf_op jit(solution)/shard_map/ppermute | solution.py:475
  10.9 5.5 %collective-permute-start.5 = (f32[256,128]{1,0:T(8,128)S(1)}, f32[256,128]{1,0:T(8,128)S(1)}, u32[]{:S(2)}, u32[]{:S(2)}) collective-permute-start(f32[256,128]{1,0:T(8,128)S(1)} %get-tuple-element.43), channel_id=1, source_target_pairs={{1,2},{2,1},{3,4},{4,3},{5,6},{6,5},{7,8},{8,7},{9,10},{10,9},{11,... | collective-permute-start | bytes 393224 | tf_op jit(solution)/shard_map/ppermute | solution.py:474
  13.1 16.9 %copy-start = (s32[1,2,3]{2,1,0:T(2,128)S(1)}, s32[1,2,3]{2,1,0:T(2,128)}, u32[]{:S(2)}) copy-start(s32[1,2,3]{2,1,0:T(2,128)} %sends.1) | copy-start | bytes 76
  14.7 15.2 %collective-permute-start.6 = (f32[256,128]{1,0:T(8,128)S(1)}, f32[256,128]{1,0:T(8,128)S(1)}, u32[]{:S(2)}, u32[]{:S(2)}) collective-permute-start(f32[256,128]{1,0:T(8,128)S(1)} %get-tuple-element.46), channel_id=1, source_target_pairs={{0,1},{1,0},{2,3},{3,2},{4,5},{5,4},{6,7},{7,6},{8,9},{9,8},{10,11... | collective-permute-start | bytes 393224 | tf_op jit(solution)/shard_map/ppermute | solution.py:475
  14.9 15.0 %collective-permute-start.7 = (f32[256,128]{1,0:T(8,128)S(1)}, f32[256,128]{1,0:T(8,128)S(1)}, u32[]{:S(2)}, u32[]{:S(2)}) collective-permute-start(f32[256,128]{1,0:T(8,128)S(1)} %get-tuple-element.47), channel_id=1, source_target_pairs={{1,2},{2,1},{3,4},{4,3},{5,6},{6,5},{7,8},{8,7},{9,10},{10,9},{11,... | collective-permute-start | bytes 393224 | tf_op jit(solution)/shard_map/ppermute | solution.py:474
